TPU v7x, 1024 devices: a whole 4x4x32 slice. The times are simulated.
1024 devices in a mesh: lev: 32 (over z), wave: 32 (over x, y, core).
Axes of the slice: x: 4, y: 4, z: 32, core: 2. Of those that a mesh axis runs over, the one named last changes fastest.
Arguments:
- legendre: float32 [320, 64, 641], P('wave'), may hold values from -0.25 to 0.25
- spectral: float32 [320, 64, 2, 641], P('wave', 'lev'), may hold values from -0.12 to 0.12
- pair_low: int32 [320], replicated, may hold values from 0 to 319, each once
- dep_lat: int32 [1280], P('wave'), may hold values from 0 to 62, as said below
- dep_col: int32 [1280], P('wave'), may hold values from 0 to 1279, as said below
- lon_steps: int32 [1280, 128], P('wave'), may hold values from 0 to 24
- tilt_steps: int32 [1280, 128], P('wave'), may hold values from 0 to 15
Outputs:
- grid_field: float32 [64, 128, 1280], P('lev', 'wave')
- departed: float32 [64, 128, 1280], P('lev', 'wave')
Inputs may be any that keep to these rules, and one draw needn't show every extreme that they name: dep_lat lies between the arrival block's own latitude index in its hemisphere minus 2 and that index plus 1, clipped to the band. dep_col is the arrival block's first column plus -3 to 3, modulo 1280.
All inputs are finite; a program needn't handle non-finite values.
Results may differ from a plain program's by a relative error of at most 0.0003.
Values sent between devices are 32-bit elements; how exact they have to be, the bound alone decides.
A program may use at most 32 MiB of HBM per device.

v0:
```python
import math

import jax
import jax.numpy as jnp
from jax import lax
from jax.sharding import PartitionSpec as P

highest = lax.Precision.HIGHEST


def with_halo(block, sides, width):
    for axis, dim in sides:
        count = lax.axis_size(axis)
        forward = [(i, i + 1) for i in range(count - 1)]
        backward = [(target, source) for source, target in forward]
        low = lax.ppermute(
            lax.slice_in_dim(block, block.shape[dim] - width, None, axis=dim), axis, forward
        )
        high = lax.ppermute(lax.slice_in_dim(block, 0, width, axis=dim), axis, backward)
        block = jnp.concatenate([low, block, high], axis=dim)
    return block


def from_behind(value, axis, by):
    count = lax.axis_size(axis)
    pairs = [(i, i + by) for i in range(count) if 0 <= i + by < count]
    return lax.ppermute(value, axis, pairs)


def legendre_sums(spectral, legendre, lower_wave, wavenumber_count):
    pair_count = spectral.shape[0]
    level_count = spectral.shape[1]
    lat_count = legendre.shape[1]
    first_len = wavenumber_count - lower_wave[:, None]
    partial_value = []
    for stride in range(2):
        spec_part = spectral[:, :, :, stride::2]
        table_part = legendre[:, :, stride::2]
        part_len = spec_part.shape[3]
        slot_pos = stride + 2 * jnp.arange(part_len, dtype=jnp.int32)
        member_one = (slot_pos[None, :] >= first_len).astype(jnp.float32)
        members = jnp.stack([1.0 - member_one, member_one], axis=1)
        masked = spec_part[:, :, :, None, :] * members[:, None, None, :, :]
        masked = masked.reshape(pair_count, level_count * 4, part_len)
        sums = jnp.einsum(
            "pak,pjk->paj",
            masked,
            table_part,
            precision=highest,
            preferred_element_type=jnp.float32,
        )
        partial_value.append(sums.reshape(pair_count, level_count, 2, 2, lat_count))
    northern = partial_value[0] + partial_value[1]
    second_sign = jnp.where(first_len[:, 0] % 2 == 0, 1.0, -1.0).astype(jnp.float32)
    south_sign = jnp.stack([jnp.ones_like(second_sign), second_sign], axis=1)
    southern = south_sign[:, None, None, :, None] * (partial_value[0] - partial_value[1])
    return jnp.stack([northern, southern], axis=4)


def fourier_rows(matrix, lower_wave, wavenumber_count):
    lon_count = 2 * wavenumber_count
    wave_table = jnp.stack([lower_wave, wavenumber_count - 1 - lower_wave], axis=0)
    gaussian_weights = jnp.where(wave_table == 0, 1.0, 2.0).astype(jnp.float32)
    lon_block = 128

    def one_block(first_lon):
        lon_ids = first_lon + jnp.arange(lon_block, dtype=jnp.int32)
        phases = wave_table[:, :, None] * lon_ids[None, None, :] % lon_count
        angles = phases.astype(jnp.float32) * (2.0 * math.pi / lon_count)
        dft_table = jnp.stack(
            [
                gaussian_weights[:, :, None] * jnp.cos(angles),
                -gaussian_weights[:, :, None] * jnp.sin(angles),
            ],
            axis=1,
        )
        dft_table = dft_table.reshape(4 * lower_wave.shape[0], lon_block)
        return jnp.dot(matrix, dft_table, precision=highest, preferred_element_type=jnp.float32)

    block_starts = jnp.arange(lon_count // lon_block, dtype=jnp.int32) * lon_block
    blocks = lax.map(one_block, block_starts)
    return jnp.moveaxis(blocks, 0, 1).reshape(matrix.shape[0], lon_count)


def mix_corners(flat_field, row_lo, row_hi, col_lo, col_hi, lon_frac, lat_frac, lon_count):

    def lookup(row_sel, col_sel):
        return jnp.take(flat_field, row_sel * lon_count + col_sel, axis=-1)

    lower_row = (1.0 - lon_frac) * lookup(row_lo, col_lo) + lon_frac * lookup(row_lo, col_hi)
    upper_row = (1.0 - lon_frac) * lookup(row_hi, col_lo) + lon_frac * lookup(row_hi, col_hi)
    return (1.0 - lat_frac) * lower_row + lat_frac * upper_row


def per_device(legendre, spectral, pair_low, dep_lat, dep_col, lon_steps, tilt_steps):
    pair_local = spectral.shape[0]
    level_count = spectral.shape[1]
    slot_count = spectral.shape[3]
    wavenumber_count = slot_count - 1
    lon_count = 2 * wavenumber_count
    lat_all = legendre.shape[1]
    wave_size = lax.axis_size("wave")
    wave_id = lax.axis_index("wave")
    lat_dev = lat_all // wave_size
    ext_rows = lat_dev + 4
    pair_total = pair_low.shape[0]
    local_low = lax.dynamic_slice_in_dim(pair_low, wave_id * pair_local, pair_local)
    sums = legendre_sums(spectral, legendre, local_low, wavenumber_count)
    arranged = sums.transpose(1, 4, 5, 3, 2, 0)
    received = lax.all_to_all(arranged, "wave", split_axis=2, concat_axis=5, tiled=True)
    matrix = received.reshape(level_count * 2 * lat_dev, 4 * pair_total)
    fourier_grid_rows = fourier_rows(matrix, pair_low, wavenumber_count).reshape(
        level_count, 2, lat_dev, lon_count
    )
    extended = with_halo(fourier_grid_rows, (("wave", 2),), 2)
    grid_field = fourier_grid_rows.reshape(level_count, 2 * lat_dev, lon_count)
    block_count = dep_lat.shape[0]
    point_count = lon_steps.shape[1]
    local_rows = jnp.arange(block_count, dtype=jnp.int32) * point_count // lon_count
    hemisphere = local_rows // lat_dev
    ext_lat = dep_lat - wave_id * lat_dev + 2
    row_lo = (hemisphere * ext_rows + ext_lat)[:, None]
    row_hi = row_lo + 1
    quarters = (
        4 * (dep_col[:, None] + jnp.arange(point_count, dtype=jnp.int32)[None, :]) + lon_steps - 12
    )
    col_lo = quarters // 4 % lon_count
    col_hi = (col_lo + 1) % lon_count
    lon_frac = (quarters % 4).astype(jnp.float32) * 0.25
    lat_frac = (tilt_steps % 4).astype(jnp.float32) * 0.25
    flat_field = extended.reshape(extended.shape[0], 2 * ext_rows * lon_count)
    horizontal = mix_corners(
        flat_field, row_lo, row_hi, col_lo, col_hi, lon_frac, lat_frac, lon_count
    )
    level_next = from_behind(horizontal[0], "lev", -1)
    is_last = lax.axis_index("lev") == lax.axis_size("lev") - 1
    level_next = jnp.where(is_last, horizontal[level_count - 1], level_next)
    upper_level = jnp.concatenate([horizontal[1:], level_next[None]], axis=0)
    vertical = (tilt_steps // 4).astype(jnp.float32) * 0.25
    departed = (1.0 - vertical) * horizontal + vertical * upper_level
    return (grid_field, departed.reshape(level_count, 2 * lat_dev, lon_count))


def solution(mesh):
    return jax.shard_map(
        per_device,
        mesh=mesh,
        in_specs=(
            P("wave", None, None),
            P("wave", "lev", None, None),
            P(),
            P("wave"),
            P("wave"),
            P("wave", None),
            P("wave", None),
        ),
        out_specs=(P("lev", "wave", None), P("lev", "wave", None)),
        check_vma=False,
    )
```

profile of v0, /device:TPU:2, one launch (start us, length us, event | category | flops | bytes accessed | tf_op | source)
XLA Modules:
  0.0 223.8 jit_solution(6442777275768511108)
XLA Ops:
  1.8 5.3 %slice.21 = f32[10,2,2,320]{3,2,1,0:T(2,128)S(1)} slice(f32[10,2,2,641]{3,2,1,0:T(2,128)} %param.12), slice={[0:10:1], [0:2:1], [0:2:1], [1:641:2]} | slice | bytes 102400 | tf_op jit(solution)/shard_map/slice | solution.py:37
  7.1 5.3 %slice.19 = f32[10,2,2,321]{3,2,1,0:T(2,128)S(1)} slice(f32[10,2,2,641]{3,2,1,0:T(2,128)} %param.12), slice={[0:10:1], [0:2:1], [0:2:1], [0:641:2]} | slice | bytes 102720 | tf_op jit(solution)/shard_map/slice | solution.py:37
  12.4 28.3 %slice.22 = f32[10,64,320]{2,1,0:T(8,128)S(1)} slice(f32[10,64,641]{2,1,0:T(8,128)} %param.11), slice={[0:10:1], [0:64:1], [1:641:2]} | slice | bytes 1638400 | tf_op jit(solution)/shard_map/slice | solution.py:38
  40.7 28.5 %slice.20 = f32[10,64,321]{2,1,0:T(8,128)S(1)} slice(f32[10,64,641]{2,1,0:T(8,128)} %param.11), slice={[0:10:1], [0:64:1], [0:641:2]} | slice | bytes 1643520 | tf_op jit(solution)/shard_map/slice | solution.py:38
  74.3 16.7 %all-to-all-start = ((f32[32,1,320]{2,1,0:T(1,128)}), f32[32,1,320]{2,1,0:T(1,128)S(1)}, u32[]{:S(2)}, u32[]{:S(2)}) async-start(f32[32,1,320]{2,1,0:T(1,128)} %reshape.405), calls=%async_computation | async-start | bytes 98304 | tf_op jit(solution)/shard_map/all_to_all | solution.py:110
  91.5 5.8 %all-to-all-done = f32[32,1,320]{2,1,0:T(1,128)S(1)} async-done(((f32[32,1,320]{2,1,0:T(1,128)}), f32[32,1,320]{2,1,0:T(1,128)S(1)}, u32[]{:S(2)}, u32[]{:S(2)}) %all-to-all-start) | async-done | bytes 40992 | tf_op jit(solution)/shard_map/all_to_all | solution.py:110
  100.0 32.0 %while.12 = (s32[]{:T(128)}, f32[10,8,128]{2,1,0:T(8,128)S(1)}, f32[2,320]{1,0:T(2,128)S(1)}, s32[2,320]{1,0:T(2,128)S(1)}, s32[10]{0:T(128)S(1)}, /*index=5*/f3...) while((s32[]{:T(128)}, f32[10,8,128]{2,1,0:T(8,128)S(1)}, f32[2,320]{1,0:T(2,128)S(1)}, ...), condition=%wide.region_1.2_spmd, body=%wide.region_0.1_spmd.sunk | while | flops 16793728 | bytes 2680433 | solution.py:81
  101.2 1.4 cosine_multiply_fusion.2
  104.4 1.4 cosine_multiply_fusion.2
  107.6 1.4 cosine_multiply_fusion.2
  110.8 1.4 cosine_multiply_fusion.2
  114.1 1.4 cosine_multiply_fusion.2
  120.5 1.4 cosine_multiply_fusion.2
  123.7 1.4 cosine_multiply_fusion.2
  126.9 1.4 cosine_multiply_fusion.2
  132.1 3.7 %collective-permute-start.1 = (f32[2,2,2,1280]{3,2,1,0:T(2,128)S(1)}, f32[2,2,2,1280]{3,2,1,0:T(2,128)S(1)}, u32[]{:S(2)}, u32[]{:S(2)}) collective-permute-start(f32[2,2,2,1280]{3,2,1,0:T(2,128)S(1)} %reshape_reshape.3), channel_id=1, source_target_pairs={{1,0},{2,1},{3,2},{4,3},{5,4},{6,5},{7,6},{8,7},{9,8},{10,9},{11,1... | collective-permute-start | bytes 122888 | tf_op jit(solution)/shard_map/ppermute | solution.py:19
  135.7 1.9 collective-permute-start
  137.8 5.4 %collective-permute-done = f32[2,2,2,1280]{3,2,1,0:T(2,128)S(1)} collective-permute-done((f32[2,2,2,1280]{3,2,1,0:T(2,128)S(1)}, f32[2,2,2,1280]{3,2,1,0:T(2,128)S(1)}, u32[]{:S(2)}, u32[]{:S(2)}) %collective-permute-start) | collective-permute-done | bytes 40992 | tf_op jit(solution)/shard_map/ppermute | solution.py:16
  143.2 4.5 %copy.47 = f32[2,2,6,1280]{0,3,2,1:T(8,128)} copy(f32[2,2,6,1280]{3,2,1,0:T(8,128)S(1)} %pad_maximum_fusion.1) | data formatting | bytes 245760 | tf_op jit(solution)/shard_map/concatenate | solution.py:20
  147.7 16.6 %gather_fusion.3 = f32[5120,2]{1,0:T(8,128)S(1)} fusion(f32[2,15360]{0,1:T(8,128)} %bitcast.92, s32[5120]{0:T(1024)S(1)} %get-tuple-element.129), kind=kCustom, calls=%fused_computation.3.clone | custom fusion | bytes 102400 | tf_op jit(solution)/shard_map/jit(_take)/gather | solution.py:88
  165.1 16.7 %gather_fusion.2 = f32[5120,2]{1,0:T(8,128)S(1)} fusion(f32[2,15360]{0,1:T(8,128)} %bitcast.93, s32[5120]{0:T(1024)S(1)} %get-tuple-element.130), kind=kCustom, calls=%fused_computation.2.clone | custom fusion | bytes 102400 | tf_op jit(solution)/shard_map/jit(_take)/gather | solution.py:88
  182.5 16.6 %gather_fusion.1 = f32[5120,2]{1,0:T(8,128)S(1)} fusion(f32[2,15360]{0,1:T(8,128)} %bitcast.94, s32[5120]{0:T(1024)S(1)} %get-tuple-element.123), kind=kCustom, calls=%fused_computation.1.clone | custom fusion | bytes 102400 | tf_op jit(solution)/shard_map/jit(_take)/gather | solution.py:88
  199.9 16.7 %gather_fusion = f32[5120,2]{1,0:T(8,128)S(1)} fusion(f32[2,15360]{0,1:T(8,128)} %bitcast.95, s32[5120]{0:T(1024)S(1)} %get-tuple-element.122), kind=kCustom, calls=%fused_computation.clone | custom fusion | bytes 102400 | tf_op jit(solution)/shard_map/jit(_take)/gather | solution.py:88
  219.4 3.7 %collective-permute-done.2 = f32[40,128]{1,0:T(8,128)S(1)} collective-permute-done((f32[40,128]{1,0:T(8,128)S(1)}, f32[40,128]{1,0:T(8,128)S(1)}, u32[]{:S(2)}, u32[]{:S(2)}) %collective-permute-start.2) | collective-permute-done | bytes 20512 | tf_op jit(solution)/shard_map/ppermute | solution.py:27
  (120 shorter events, 35.1 us)
Async XLA Ops:
  69.6 21.4 %copy-start.1 = (s32[320]{0:T(512)S(1)}, s32[320]{0:T(512)}, u32[]{:S(2)}) copy-start(s32[320]{0:T(512)} %param.13) | copy-start | bytes 3844
  69.6 21.5 %copy-start.4 = (s32[40]{0:T(128)S(1)}, s32[40]{0:T(128)}, u32[]{:S(2)}) copy-start(s32[40]{0:T(128)} %param.14) | copy-start | bytes 484
  69.7 21.5 %copy-start = (s32[40,128]{1,0:T(8,128)S(1)}, s32[40,128]{1,0:T(8,128)}, u32[]{:S(2)}) copy-start(s32[40,128]{1,0:T(8,128)} %param.16) | copy-start | bytes 61444
  69.7 21.5 %copy-start.3 = (s32[40]{0:T(128)S(1)}, s32[40]{0:T(128)}, u32[]{:S(2)}) copy-start(s32[40]{0:T(128)} %param.15) | copy-start | bytes 484
  69.7 21.6 %copy-start.2 = (s32[40,128]{1,0:T(8,128)S(1)}, s32[40,128]{1,0:T(8,128)}, u32[]{:S(2)}) copy-start(s32[40,128]{1,0:T(8,128)} %param.17) | copy-start | bytes 61444
  74.3 23.1 %all-to-all-start = ((f32[32,1,320]{2,1,0:T(1,128)}), f32[32,1,320]{2,1,0:T(1,128)S(1)}, u32[]{:S(2)}, u32[]{:S(2)}) async-start(f32[32,1,320]{2,1,0:T(1,128)} %reshape.405), calls=%async_computation | async-start | bytes 98304 | tf_op jit(solution)/shard_map/all_to_all | solution.py:110
  132.1 5.7 %collective-permute-start.1 = (f32[2,2,2,1280]{3,2,1,0:T(2,128)S(1)}, f32[2,2,2,1280]{3,2,1,0:T(2,128)S(1)}, u32[]{:S(2)}, u32[]{:S(2)}) collective-permute-start(f32[2,2,2,1280]{3,2,1,0:T(2,128)S(1)} %reshape_reshape.3), channel_id=1, source_target_pairs={{1,0},{2,1},{3,2},{4,3},{5,4},{6,5},{7,6},{8,7},{9,8},{10,9},{11,1... | collective-permute-start | bytes 122888 | tf_op jit(solution)/shard_map/ppermute | solution.py:19
  135.7 7.4 %collective-permute-start = (f32[2,2,2,1280]{3,2,1,0:T(2,128)S(1)}, f32[2,2,2,1280]{3,2,1,0:T(2,128)S(1)}, u32[]{:S(2)}, u32[]{:S(2)}) collective-permute-start(f32[2,2,2,1280]{3,2,1,0:T(2,128)S(1)} %reshape_reshape.3), channel_id=1, source_target_pairs={{0,1},{1,2},{2,3},{3,4},{4,5},{5,6},{6,7},{7,8},{8,9},{9,10},{10,1... | collective-permute-start | bytes 122888 | tf_op jit(solution)/shard_map/ppermute | solution.py:16
  217.4 5.7 %collective-permute-start.2 = (f32[40,128]{1,0:T(8,128)S(1)}, f32[40,128]{1,0:T(8,128)S(1)}, u32[]{:S(2)}, u32[]{:S(2)}) collective-permute-start(f32[40,128]{1,0:T(8,128)S(1)} %get-tuple-element.119), channel_id=1, source_target_pairs={{32,0},{64,32},{96,64},{128,96},{160,128},{192,160},{224,192},{256... | collective-permute-start | bytes 61448 | tf_op jit(solution)/shard_map/ppermute | solution.py:27
where the time goes:
time: 225 us; the launch traced here: 224 us
  local copies, waits for them, and re-layouts  153 us (68%)
  other arithmetic  24.1 us (11%)
  starting transfers between devices  23.6 us (10%)
  waiting for transfers between devices  15 us (7%)
  matrix products  6.85 us (3%)
    gather x8, local copies, waits for them, and re-layouts, lookup(): return jnp.take(flat_field, row_sel * lon_count + col_sel, axis=-1)  69.6 us
    slice x2, local copies, waits for them, and re-layouts, legendre_sums(): table_part = legendre[:, :, stride::2]  56.9 us
    all_to_all x1, starting transfers between devices, per_device(): lax.all_to_all(arranged, 'wave', split_axis=2, concat_axis=5, tiled=True)  16.7 us
    mul x10, other arithmetic, one_block(): gaussian_weights[:, :, None] * jnp.cos(angles)  14.3 us
    slice x2, local copies, waits for them, and re-layouts, legendre_sums(): spec_part = spectral[:, :, :, stride::2]  10.6 us
    add x10, other arithmetic, one_block(): lon_ids = first_lon + jnp.arange(lon_block, dtype=jnp.int32)  6.47 us
    dynamic_slice x10, local copies, waits for them, and re-layouts, fourier_rows(): blocks = lax.map(one_block, block_starts)  5.92 us
    all_to_all x1, waiting for transfers between devices, per_device(): lax.all_to_all(arranged, 'wave', split_axis=2, concat_axis=5, tiled=True)  5.83 us
  transfers between devices with their start and end apart: 4, of which 3 were waited for; matrix products, arithmetic and copies ran while one was open for 0% of the time, Pallas kernels for 0%

commit v1 on v0

v1 whole, which is shorter than its diff:
```python
import functools
import math

import jax
import jax.numpy as jnp
import numpy as np
from jax import lax
from jax.experimental import pallas as pl
from jax.experimental.pallas import tpu as pltpu
from jax.sharding import PartitionSpec as P

MESH = pl.DeviceIdType.MESH
NT = (((1,), (1,)), ((), ()))
f32 = jnp.float32
bf16 = jnp.bfloat16


def split(x):
    hi = x.astype(bf16)
    lo = (x - hi.astype(f32)).astype(bf16)
    return hi, lo


def legendre_into(send_ref, low_of, leg_ref, spec_ref, wait_pair, y_ref, z_ref, turn):
    pairs, lats, slots = leg_ref.shape
    top = slots - 1
    k = lax.broadcasted_iota(jnp.int32, (8, slots), 1)
    row = lax.broadcasted_iota(jnp.int32, (8, slots), 0)
    hemi, member, part = row // 4, (row // 2) % 2, row % 2
    y_ref[...] = jnp.zeros_like(y_ref)
    send_ref[0] = jnp.zeros(send_ref.shape[1:], f32)
    send_ref[lats // 2 + 1] = jnp.zeros(send_ref.shape[1:], f32)
    for s in range(pairs):
        wait_pair(s)
        first = top - low_of(s)
        keep = (k >= first) == (member == 1)
        odd = (k + member * first) % 2
        mask = jnp.where(keep, 1 - 2 * (hemi * odd), 0).astype(f32)
        rows = []
        for lev in range(2):
            re = jnp.broadcast_to(spec_ref[s, lev, 0:1, :], (8, slots))
            im = jnp.broadcast_to(spec_ref[s, lev, 1:2, :], (8, slots))
            rows.append(jnp.where(part == 0, re, im) * mask)
        hi, lo = split(jnp.concatenate(rows, axis=0))
        leg_hi, leg_lo = split(leg_ref[s])
        both = lax.dot_general(jnp.concatenate([hi, lo], axis=0), leg_hi, NT, preferred_element_type=f32)
        small = lax.dot_general(hi, leg_lo, NT, preferred_element_type=f32)
        y_ref[pl.ds(s, 16, stride=16), :] = both[:16] + (both[16:] + small)
    lane = lax.broadcasted_iota(jnp.int32, (lats // 2, 128), 1)
    for lev in range(2):
        z_ref[...] = y_ref[pl.ds(128 * lev, 128), :].T
        even = z_ref[pl.ds(0, lats // 2, stride=2), :]
        odd = z_ref[pl.ds(1, lats // 2, stride=2), :]
        for h in range(2):
            if h == 0:
                val = jnp.where(lane < 64, even, pltpu.roll(odd, 64, 1))
            else:
                val = jnp.where(lane < 64, pltpu.roll(even, 64, 1), odd)
            val = pltpu.roll(val, 16 * turn, 1)
            for j in range(lats // 2):
                send_ref[1 + j, lev, h : h + 1, :] = val[j : j + 1, :]


def exchange_kernel(
    waves, levs, low_ref, leg_hbm, spec_hbm, recv_ref,
    leg_ref, spec_ref, y_ref, z_ref, send_ref,
    leg_sem, spec_sem, self_sem, send_sem, recv_sem, up_send_sem, up_recv_sem,
):
    me = lax.axis_index("wave")
    lev = lax.axis_index("lev")
    above = lax.rem(lev + 1, levs)
    below = lax.rem(lev + levs - 1, levs)
    pairs = leg_ref.shape[0]
    spec_copy = pltpu.make_async_copy(spec_hbm, spec_ref, spec_sem)
    spec_copy.start()
    leg_copies = [
        pltpu.make_async_copy(leg_hbm.at[s], leg_ref.at[s], leg_sem.at[s]) for s in range(pairs)
    ]
    for copy in leg_copies:
        copy.start()

    barrier = pltpu.get_barrier_semaphore()

    def greet(d, _):
        pl.semaphore_signal(barrier, inc=1, device_id={"lev": lev, "wave": lax.rem(me + d, waves)}, device_id_type=MESH)
        return 0

    def greet_above(w, _):
        pl.semaphore_signal(barrier, inc=1, device_id={"lev": above, "wave": w}, device_id_type=MESH)
        return 0

    lax.fori_loop(1, waves, greet, 0)
    lax.fori_loop(0, waves, greet_above, 0)

    def wait_pair(s):
        if s == 0:
            spec_copy.wait()
        leg_copies[s].wait()

    legendre_into(
        send_ref, lambda s: low_ref[me * pairs + s], leg_ref, spec_ref, wait_pair, y_ref, z_ref,
        lax.rem(me, 8),
    )
    pl.semaphore_wait(barrier, 2 * waves - 1)

    def across(peer, sender):
        return pltpu.make_async_remote_copy(
            src_ref=send_ref.at[pl.ds(peer, 3)],
            dst_ref=recv_ref.at[sender, :, pl.ds(0, 2)],
            send_sem=send_sem.at[peer],
            recv_sem=recv_sem.at[sender],
            device_id={"lev": lev, "wave": peer},
            device_id_type=MESH,
        )

    def down(peer, sender):
        return pltpu.make_async_remote_copy(
            src_ref=send_ref.at[pl.ds(peer, 3), 0],
            dst_ref=recv_ref.at[sender, :, 2],
            send_sem=up_send_sem.at[peer],
            recv_sem=up_recv_sem.at[sender],
            device_id={"lev": below, "wave": peer},
            device_id_type=MESH,
        )

    def start(d, _):
        peer = lax.rem(me + d, waves)
        down(peer, me).start()

        @pl.when(d > 0)
        def _():
            across(peer, me).start()

        return 0

    lax.fori_loop(0, waves, start, 0)
    own = pltpu.make_async_copy(send_ref.at[pl.ds(me, 3)], recv_ref.at[me, :, pl.ds(0, 2)], self_sem)
    own.start()
    own.wait()

    def finish(d, _):
        peer = lax.rem(me + d, waves)
        down(peer, peer).wait_recv()
        down(peer, me).wait_send()

        @pl.when(d > 0)
        def _():
            across(peer, peer).wait_recv()
            across(peer, me).wait_send()

        return 0

    lax.fori_loop(0, waves, finish, 0)


def exchange(pair_low, legendre, spectral, waves, levs):
    pairs, lats, slots = legendre.shape
    any_space = pl.BlockSpec(memory_space=pl.ANY)
    return pl.pallas_call(
        functools.partial(exchange_kernel, waves, levs),
        out_shape=jax.ShapeDtypeStruct((waves, 3, 4, 2, 128), f32),
        in_specs=[pl.BlockSpec(memory_space=pltpu.SMEM), any_space, any_space],
        out_specs=pl.BlockSpec(memory_space=pltpu.VMEM),
        scratch_shapes=[
            pltpu.VMEM((pairs, lats, slots), f32),
            pltpu.VMEM(spectral.shape, f32),
            pltpu.VMEM((256, lats), f32),
            pltpu.VMEM((lats, 128), f32),
            pltpu.VMEM((lats // 2 + 2, 2, 2, 128), f32),
            pltpu.SemaphoreType.DMA((pairs,)),
            pltpu.SemaphoreType.DMA,
            pltpu.SemaphoreType.DMA,
            pltpu.SemaphoreType.DMA((waves,)),
            pltpu.SemaphoreType.DMA((waves,)),
            pltpu.SemaphoreType.DMA((waves,)),
            pltpu.SemaphoreType.DMA((waves,)),
        ],
        compiler_params=pltpu.CompilerParams(collective_id=0, has_side_effects=True),
    )(pair_low, legendre, spectral)


def spread_low(low_ref):
    lane = lax.broadcasted_iota(jnp.int32, (8, 128), 1)
    parts = [jnp.broadcast_to(low_ref[pl.ds(128 * v, 128)].reshape(1, 128), (8, 128)) for v in range(3)]
    out = []
    for v in range(4):
        source = 80 * v + 10 * (lane // 16) + lane % 16
        first = 80 * v // 128
        last = (80 * v + 79) // 128
        got = jnp.take_along_axis(parts[first], source % 128, axis=1)
        if last != first:
            other = jnp.take_along_axis(parts[last], source % 128, axis=1)
            got = jnp.where(source // 128 == first, got, other)
        out.append(jnp.where(lane % 16 < 10, got, -1))
    return out


def order_into(order_ref, low_ref, top):
    low = spread_low(low_ref)
    columns = order_ref.shape[1]
    for e in range(2):
        for n0 in range(0, columns, 16):
            g, q, mu0 = n0 // 128, n0 % 128 // 32, n0 % 32
            p = 4 * g + q
            row = lax.broadcasted_iota(jnp.int32, (8, 128), 0)
            halves = []
            for half in range(2):
                m = p + 10 * (32 * e + mu0 + 8 * half + row)
                want = m if e == 0 else top - 1 - m
                weight = jnp.where(m == 0, 1.0, 2.0) if (e == 0 and p == 0) else jnp.full((8, 128), 2.0, f32)
                halves.append((want, weight))
            for v in range(4):
                if p >= 10:
                    block = jnp.zeros((16, 128), f32)
                else:
                    block = jnp.concatenate(
                        [jnp.where(low[v] == want, weight, 0.0) for want, weight in halves], axis=0
                    )
                order_ref[e, pl.ds(n0, 16), pl.ds(128 * v, 128)] = block.astype(bf16)


def grid_kernel(
    low_ref, lat_ref, col_ref, recv_ref, lon_ref, tilt_ref, table_hi_ref, table_lo_ref, twiddle_ref,
    grid_ref, departed_ref, order_ref, x_ref, field_ref, edge_ref, levs,
):
    wave = lax.axis_index("wave")
    last = lax.axis_index("lev") == levs - 1
    top = 640
    order_into(order_ref, low_ref, top)

    lane = lax.broadcasted_iota(jnp.int32, (8, 128), 1)
    slot = lane // 16
    for grp in range(4):
        for t in range(3):
            arr = [recv_ref[8 * grp + j, t] for j in range(8)]
            for bit in range(3):
                step = 1 << bit
                on = (slot & step) != 0
                arr = [jnp.where(on, arr[(j + step) % 8], arr[j]) for j in range(8)]
            for e in range(2):
                for r in range(2):
                    pieces = []
                    for l in range(2):
                        c = 4 * l + 2 * e + r
                        pieces.append(pltpu.roll(arr[-c % 8], (128 - 16 * c) % 128, 1))
                    hi, lo = split(jnp.concatenate(pieces, axis=0))
                    cols = pl.ds(128 * grp, 128)
                    x_ref[e, pl.ds(48 * r + 16 * t, 16), cols] = hi
                    x_ref[e, pl.ds(96 + 48 * r + 16 * t, 16), cols] = lo

    sums = []
    for e in range(2):
        both = lax.dot_general(x_ref[e], order_ref[e], NT, preferred_element_type=f32)
        sums.append(both[:96] + both[96:])

    slot48 = lax.broadcasted_iota(jnp.int32, (48, 128), 1) // 32
    by_q = [[] for _ in range(4)]
    for g in range(3):
        arr = []
        for i in range(4):
            block = sums[i // 2][48 * (i % 2) : 48 * (i % 2) + 48, 128 * g : 128 * g + 128]
            arr.append(pltpu.roll(block, 32 * i, 1) if i else block)
        for bit in range(2):
            step = 1 << bit
            on = (slot48 & step) != 0
            arr = [jnp.where(on, arr[(j + step) % 4], arr[j]) for j in range(4)]
        for q in range(4):
            if 4 * g + q < 10:
                by_q[q].append(arr[-q % 4])
    re, im = [None] * 10, [None] * 10
    for q in range(4):
        n = 48 * len(by_q[q])
        hi, lo = split(jnp.concatenate(by_q[q], axis=0))
        rows = pl.ds(32 * (-q % 4), 128)
        both = jnp.dot(jnp.concatenate([hi, lo], axis=0), table_hi_ref[rows, :], preferred_element_type=f32)
        small = jnp.dot(hi, table_lo_ref[rows, :], preferred_element_type=f32)
        total = both[:n] + (both[n:] + small)
        for g in range(len(by_q[q])):
            p = 4 * g + q
            a, b = total[48 * g : 48 * g + 48, :128], total[48 * g : 48 * g + 48, 128:]
            if p == 0:
                re[p], im[p] = a, b
            else:
                c = twiddle_ref[2 * p : 2 * p + 1, :]
                s = twiddle_ref[2 * p + 1 : 2 * p + 2, :]
                re[p] = a * c - b * s
                im[p] = a * s + b * c

    def put(x, value):
        field_ref[x] = value

    even = [re[p] + re[10 - p] for p in (1, 2, 3, 4)]
    diff = [im[p] - im[10 - p] for p in (1, 2, 3, 4)]
    for x in range(3):
        co = [math.cos(math.pi * p * x / 5) for p in (1, 2, 3, 4)]
        si = [math.sin(math.pi * p * x / 5) for p in (1, 2, 3, 4)]
        if x == 0:
            a_even = re[0] + (even[1] + even[3])
            a_odd = re[5] + (even[0] + even[2])
            put(0, a_even + a_odd)
            put(5, a_even - a_odd)
            continue
        a_even = re[0] + (co[1] * even[1] + co[3] * even[3])
        a_odd = (co[0] * even[0] + co[2] * even[2]) + (re[5] if x % 2 == 0 else -re[5])
        b_even = si[1] * diff[1] + si[3] * diff[3]
        b_odd = si[0] * diff[0] + si[2] * diff[2]
        a, b = a_even + a_odd, b_even + b_odd
        put(x, a - b)
        put(10 - x, a + b)
        a, b = a_even - a_odd, b_odd - b_even
        put(5 - x, a - b)
        put(5 + x, a + b)

    lane48 = lax.broadcasted_iota(jnp.int32, (48, 128), 1)
    for x in range(10):
        edge_ref[x] = jnp.where(lane48 < 64, field_ref[(x + 1) % 10], field_ref[(x + 9) % 10])
        for l in range(2):
            for row in range(4):
                lev, h = row // 2, row % 2
                grid_ref[lev, pl.ds(2 * h + l, 1), pl.ds(128 * x, 128)] = field_ref[x, pl.ds(8 * (2 + l) + row, 1), :]

    hemi = lax.broadcasted_iota(jnp.int32, (8, 128), 0) % 2 == 1
    keep_own = jnp.logical_and(last, lax.broadcasted_iota(jnp.int32, (8, 128), 0) >= 2)
    for l in range(2):
        for x in range(10):
            north, south = 10 * l + x, 20 + 10 * l + x

            def pick(ref):
                return jnp.where(
                    hemi,
                    jnp.broadcast_to(ref[south : south + 1, :], (8, 128)),
                    jnp.broadcast_to(ref[north : north + 1, :], (8, 128)),
                )

            lon, tilt = pick(lon_ref), pick(tilt_ref)

            def shift_of(block):
                return lax.rem(col_ref[block] - 128 * x + 1280 + 640, 1280) - 640

            base = jnp.where(hemi, shift_of(south), shift_of(north))
            index = lane + base + (lon >> 2) - 3
            nxt = index + 1
            frac = (lon & 3).astype(f32) * 0.25
            g = (tilt & 3).astype(f32) * 0.25
            v = (tilt >> 2).astype(f32) * 0.25
            rows = []
            for off in range(2):
                starts = [
                    pl.multiple_of(8 * (lat_ref[block] - 2 * wave + 2 + off), 8) for block in (north, south)
                ]
                main = jnp.where(hemi, field_ref[x, pl.ds(starts[1], 8), :], field_ref[x, pl.ds(starts[0], 8), :])
                edge = jnp.where(hemi, edge_ref[x, pl.ds(starts[1], 8), :], edge_ref[x, pl.ds(starts[0], 8), :])

                def look(at):
                    inside = (at >> 7) == 0
                    return jnp.where(
                        inside,
                        jnp.take_along_axis(main, at & 127, axis=1),
                        jnp.take_along_axis(edge, at & 127, axis=1),
                    )

                rows.append((1.0 - frac) * look(index) + frac * look(nxt))
            horizontal = (1.0 - g) * rows[0] + g * rows[1]
            upper = jnp.where(keep_own, horizontal, pltpu.roll(horizontal, 6, 0))
            departed = (1.0 - v) * horizontal + v * upper
            for row in range(4):
                lev, h = row // 2, row % 2
                departed_ref[lev, pl.ds(2 * h + l, 1), pl.ds(128 * x, 128)] = departed[row : row + 1, :]


def dft_tables():
    slot = np.arange(224) // 32 % 4
    member, part = slot // 2, slot % 2
    m2 = 32 * member + np.arange(224) % 32
    x = np.arange(128)
    theta = 2 * np.pi * ((m2[:, None] * x[None, :]) % 128) / 128
    c, s = np.cos(theta), np.sin(theta)
    part = part[:, None]
    table = np.concatenate([np.where(part == 0, c, -s), np.where(part == 0, s, c)], axis=1)
    hi = table.astype(jnp.bfloat16)
    lo = (table - hi.astype(np.float64)).astype(jnp.bfloat16)
    angle = 2 * np.pi * np.arange(10)[:, None] * x[None, :] / 1280
    twiddle = np.stack([np.cos(angle), np.sin(angle)], axis=1).reshape(20, 128).astype(np.float32)
    return hi, lo, twiddle


def to_grid(pair_low, dep_lat, dep_col, received, lon_steps, tilt_steps, levs):
    hi, lo, twiddle = dft_tables()
    vmem = pl.BlockSpec(memory_space=pltpu.VMEM)
    smem = pl.BlockSpec(memory_space=pltpu.SMEM)

    def kernel(*refs):
        grid_kernel(*refs, levs)

    low = jnp.pad(pair_low, (0, 64), constant_values=-1)
    return pl.pallas_call(
        kernel,
        out_shape=[jax.ShapeDtypeStruct((2, 4, 1280), f32)] * 2,
        in_specs=[vmem, smem, smem] + [vmem] * 6,
        out_specs=[vmem, vmem],
        scratch_shapes=[
            pltpu.VMEM((2, 384, 512), bf16),
            pltpu.VMEM((2, 192, 512), bf16),
            pltpu.VMEM((10, 48, 128), f32),
            pltpu.VMEM((10, 48, 128), f32),
        ],
        name="grid",
    )(low, dep_lat, dep_col, received, lon_steps, tilt_steps, jnp.asarray(hi), jnp.asarray(lo), jnp.asarray(twiddle))


def per_device(legendre, spectral, pair_low, dep_lat, dep_col, lon_steps, tilt_steps):
    waves, levs = lax.axis_size("wave"), lax.axis_size("lev")
    received = exchange(pair_low, legendre, spectral, waves, levs).reshape(waves, 3, 8, 128)
    return tuple(to_grid(pair_low, dep_lat, dep_col, received, lon_steps, tilt_steps, levs))


def solution(mesh):
    return jax.shard_map(
        per_device,
        mesh=mesh,
        in_specs=(
            P("wave", None, None),
            P("wave", "lev", None, None),
            P(),
            P("wave"),
            P("wave"),
            P("wave", None),
            P("wave", None),
        ),
        out_specs=(P("lev", "wave", None), P("lev", "wave", None)),
        check_vma=False,
    )
```

time: 225 us -> 37.2 us (0.17)
  the two profiles are of different devices: /device:TPU:2 before, /device:TPU:1 now
where the time goes in v1:
time: 37.2 us; the launch traced here: 36.9 us
  Pallas kernels  35 us (94%)
  local copies, waits for them, and re-layouts  1.26 us (3%)
  between operations  0.64 us (2%)
    pallas_call x1, Pallas kernels, exchange(): pl.pallas_call(functools.partial(exchange_kernel, waves, levs), out_shape...  31.8 us
    pallas_call x1, Pallas kernels, to_grid(): pl.pallas_call(kernel, out_shape=[jax.ShapeDtypeStruct((2, 4, 1280), f32)...  3.23 us
    pad x1, local copies, waits for them, and re-layouts, to_grid(): low = jnp.pad(pair_low, (0, 64), constant_values=-1)  1.26 us

profile of v1, /device:TPU:1, one launch (start us, length us, event | category | flops | bytes accessed | tf_op | source)
XLA Modules:
  0.0 36.9 jit_solution(9483593534941157826)
XLA Ops:
  0.6 1.3 %pad.4.refs_0_ = s32[384]{0:T(512)} pad(s32[320]{0:T(512)} %low_ref.1, s32[]{:T(128)} %constant.3.clone.1), padding=0_64 | pad | bytes 2820 | tf_op jit(solution)/shard_map/jit(_pad)/pad | solution.py:395
  1.9 31.8 %shard_map.113 = f32[32,3,4,2,128]{4,3,2,1,0:T(2,128)} custom-call(s32[320]{0:T(512)} %low_ref.1, f32[10,64,641]{2,1,0:T(8,128)} %leg_hbm.1, f32[10,2,2,641]{3,2,1,0:T(2,128)} %spec_hbm.1), custom_call_target="tpu_custom_call" | custom-call | tf_op jit(solution)/shard_map/pallas_call | solution.py:159
  33.7 3.2 %grid.1 = (f32[2,4,1280]{2,1,0:T(4,128)}, f32[2,4,1280]{2,1,0:T(4,128)}) custom-call(s32[384]{0:T(512)} %pad.4.refs_0_, s32[40]{0:T(128)} %refs_1_.1, s32[40]{0:T(128)} %refs_2_.1, f32[32,3,8,128]{3,2,1,0:T(8,128)} %bitcast.1, s32[40,128]{1,0:T(8,128)} %refs_4_.1, s32[40,128]{1,0:T(8,128)} %refs_5_.1, bf16[224,256]{1,0:T(8,128)(2,1)} %constant.8.clone.refs_6_, ...), custom_call_target="tpu_custom_call" | custom-call | tf_op jit(solution)/shard_map/grid/pallas_call | solution.py:396

commit v2 on v1

--- a/solution.py
+++ b/solution.py
@@ -10,6 +10,7 @@
 from jax.sharding import PartitionSpec as P
 
 MESH = pl.DeviceIdType.MESH
+LIMIT = 16 * 1024 * 1024
 NT = (((1,), (1,)), ((), ()))
 f32 = jnp.float32
 bf16 = jnp.bfloat16
@@ -62,15 +63,15 @@
 
 
 def exchange_kernel(
-    waves, levs, low_ref, leg_hbm, spec_hbm, recv_ref,
-    leg_ref, spec_ref, y_ref, z_ref, send_ref,
-    leg_sem, spec_sem, self_sem, send_sem, recv_sem, up_send_sem, up_recv_sem,
+    waves, levs, low_hbm, leg_hbm, spec_hbm, recv_ref, order_ref,
+    low_smem, low_vmem, leg_ref, spec_ref, y_ref, z_ref, send_ref,
+    low_sem, leg_sem, spec_sem, send_sem, recv_sem, down_send_sem, down_recv_sem,
 ):
     me = lax.axis_index("wave")
     lev = lax.axis_index("lev")
-    above = lax.rem(lev + 1, levs)
-    below = lax.rem(lev + levs - 1, levs)
-    pairs = leg_ref.shape[0]
+    pairs, _, slots = leg_ref.shape
+    low_copy = pltpu.make_async_copy(low_hbm, low_smem, low_sem.at[0])
+    low_copy.start()
     spec_copy = pltpu.make_async_copy(spec_hbm, spec_ref, spec_sem)
     spec_copy.start()
     leg_copies = [
@@ -78,6 +79,8 @@
     ]
     for copy in leg_copies:
         copy.start()
+    low_again = pltpu.make_async_copy(low_hbm, low_vmem, low_sem.at[1])
+    low_again.start()
 
     barrier = pltpu.get_barrier_semaphore()
 
@@ -86,11 +89,16 @@
         return 0
 
     def greet_above(w, _):
-        pl.semaphore_signal(barrier, inc=1, device_id={"lev": above, "wave": w}, device_id_type=MESH)
+        pl.semaphore_signal(barrier, inc=1, device_id={"lev": lev + 1, "wave": w}, device_id_type=MESH)
         return 0
 
     lax.fori_loop(1, waves, greet, 0)
-    lax.fori_loop(0, waves, greet_above, 0)
+
+    @pl.when(lev < levs - 1)
+    def _():
+        lax.fori_loop(0, waves, greet_above, 0)
+
+    low_copy.wait()
 
     def wait_pair(s):
         if s == 0:
@@ -98,98 +106,110 @@
         leg_copies[s].wait()
 
     legendre_into(
-        send_ref, lambda s: low_ref[me * pairs + s], leg_ref, spec_ref, wait_pair, y_ref, z_ref,
+        send_ref, lambda s: low_smem[me * pairs + s], leg_ref, spec_ref, wait_pair, y_ref, z_ref,
         lax.rem(me, 8),
     )
-    pl.semaphore_wait(barrier, 2 * waves - 1)
-
-    def across(peer, sender):
-        return pltpu.make_async_remote_copy(
+    pl.semaphore_wait(barrier, waves - 1 + jnp.where(lev > 0, waves, 0))
+
+    def across(d, _):
+        peer = lax.rem(me + d, waves)
+        pltpu.make_async_remote_copy(
             src_ref=send_ref.at[pl.ds(peer, 3)],
-            dst_ref=recv_ref.at[sender, :, pl.ds(0, 2)],
-            send_sem=send_sem.at[peer],
-            recv_sem=recv_sem.at[sender],
+            dst_ref=recv_ref.at[me, :, pl.ds(0, 2)],
+            send_sem=send_sem,
+            recv_sem=recv_sem,
             device_id={"lev": lev, "wave": peer},
             device_id_type=MESH,
-        )
-
-    def down(peer, sender):
-        return pltpu.make_async_remote_copy(
+        ).start()
+        return 0
+
+    def down(d, _):
+        peer = lax.rem(me + d, waves)
+        pltpu.make_async_remote_copy(
             src_ref=send_ref.at[pl.ds(peer, 3), 0],
-            dst_ref=recv_ref.at[sender, :, 2],
-            send_sem=up_send_sem.at[peer],
-            recv_sem=up_recv_sem.at[sender],
-            device_id={"lev": below, "wave": peer},
+            dst_ref=recv_ref.at[me, :, 2],
+            send_sem=down_send_sem,
+            recv_sem=down_recv_sem,
+            device_id={"lev": lev - 1, "wave": peer},
             device_id_type=MESH,
-        )
-
-    def start(d, _):
-        peer = lax.rem(me + d, waves)
-        down(peer, me).start()
-
-        @pl.when(d > 0)
-        def _():
-            across(peer, me).start()
-
+        ).start()
         return 0
 
-    lax.fori_loop(0, waves, start, 0)
-    own = pltpu.make_async_copy(send_ref.at[pl.ds(me, 3)], recv_ref.at[me, :, pl.ds(0, 2)], self_sem)
+    lax.fori_loop(1, waves, across, 0)
+
+    @pl.when(lev > 0)
+    def _():
+        lax.fori_loop(0, waves, down, 0)
+
+    own = pltpu.make_async_copy(send_ref.at[pl.ds(me, 3)], recv_ref.at[me, :, pl.ds(0, 2)], recv_sem)
     own.start()
-    own.wait()
-
-    def finish(d, _):
-        peer = lax.rem(me + d, waves)
-        down(peer, peer).wait_recv()
-        down(peer, me).wait_send()
-
-        @pl.when(d > 0)
-        def _():
-            across(peer, peer).wait_recv()
-            across(peer, me).wait_send()
-
-        return 0
-
-    lax.fori_loop(0, waves, finish, 0)
+    low_again.wait()
+    order_into(order_ref, low_vmem, slots - 1)
+
+    all_across = recv_ref.at[:, :, pl.ds(0, 2)]
+    sent_across = recv_ref.at[pl.ds(0, waves - 1), :, pl.ds(0, 2)]
+    all_down = recv_ref.at[:, :, 2]
+    pltpu.make_async_copy(all_across, all_across, recv_sem).wait()
+
+    @pl.when(lev < levs - 1)
+    def _():
+        pltpu.make_async_copy(all_down, all_down, down_recv_sem).wait()
+
+    pltpu.make_async_copy(sent_across, sent_across, send_sem).wait()
+
+    @pl.when(lev > 0)
+    def _():
+        pltpu.make_async_copy(all_down, all_down, down_send_sem).wait()
 
 
 def exchange(pair_low, legendre, spectral, waves, levs):
     pairs, lats, slots = legendre.shape
-    any_space = pl.BlockSpec(memory_space=pl.ANY)
+    any_space = pl.BlockSpec(memory_space=pltpu.HBM)
+    vmem = pl.BlockSpec(memory_space=pltpu.VMEM)
     return pl.pallas_call(
         functools.partial(exchange_kernel, waves, levs),
-        out_shape=jax.ShapeDtypeStruct((waves, 3, 4, 2, 128), f32),
-        in_specs=[pl.BlockSpec(memory_space=pltpu.SMEM), any_space, any_space],
-        out_specs=pl.BlockSpec(memory_space=pltpu.VMEM),
+        out_shape=[
+            jax.ShapeDtypeStruct((waves, 3, 4, 2, 128), f32),
+            jax.ShapeDtypeStruct((2, 384, 512), bf16),
+        ],
+        in_specs=[any_space] * 3,
+        out_specs=[vmem, vmem],
         scratch_shapes=[
+            pltpu.SMEM(pair_low.shape, jnp.int32),
+            pltpu.VMEM(pair_low.shape, jnp.int32),
             pltpu.VMEM((pairs, lats, slots), f32),
             pltpu.VMEM(spectral.shape, f32),
             pltpu.VMEM((256, lats), f32),
             pltpu.VMEM((lats, 128), f32),
             pltpu.VMEM((lats // 2 + 2, 2, 2, 128), f32),
+            pltpu.SemaphoreType.DMA((2,)),
             pltpu.SemaphoreType.DMA((pairs,)),
             pltpu.SemaphoreType.DMA,
             pltpu.SemaphoreType.DMA,
-            pltpu.SemaphoreType.DMA((waves,)),
-            pltpu.SemaphoreType.DMA((waves,)),
-            pltpu.SemaphoreType.DMA((waves,)),
-            pltpu.SemaphoreType.DMA((waves,)),
+            pltpu.SemaphoreType.DMA,
+            pltpu.SemaphoreType.DMA,
+            pltpu.SemaphoreType.DMA,
         ],
-        compiler_params=pltpu.CompilerParams(collective_id=0, has_side_effects=True),
-    )(pair_low, legendre, spectral)
+        compiler_params=pltpu.CompilerParams(
+            collective_id=0, has_side_effects=True, vmem_limit_bytes=LIMIT
+        ),
+    )(*[pltpu.with_memory_space_constraint(a, pltpu.HBM) for a in (pair_low, legendre, spectral)])
 
 
 def spread_low(low_ref):
     lane = lax.broadcasted_iota(jnp.int32, (8, 128), 1)
-    parts = [jnp.broadcast_to(low_ref[pl.ds(128 * v, 128)].reshape(1, 128), (8, 128)) for v in range(3)]
+    row = low_ref[...].reshape(1, low_ref.shape[0])
+    ends = [(0, 128), (128, 256), (192, 320)]
+    parts = [jnp.broadcast_to(row[:, a:b], (8, 128)) for a, b in ends]
     out = []
     for v in range(4):
         source = 80 * v + 10 * (lane // 16) + lane % 16
         first = 80 * v // 128
         last = (80 * v + 79) // 128
-        got = jnp.take_along_axis(parts[first], source % 128, axis=1)
+        shift = [0, 0, 64]
+        got = jnp.take_along_axis(parts[first], (source + shift[first]) % 128, axis=1)
         if last != first:
-            other = jnp.take_along_axis(parts[last], source % 128, axis=1)
+            other = jnp.take_along_axis(parts[last], (source + shift[last]) % 128, axis=1)
             got = jnp.where(source // 128 == first, got, other)
         out.append(jnp.where(lane % 16 < 10, got, -1))
     return out
@@ -220,13 +240,15 @@
 
 
 def grid_kernel(
-    low_ref, lat_ref, col_ref, recv_ref, lon_ref, tilt_ref, table_hi_ref, table_lo_ref, twiddle_ref,
-    grid_ref, departed_ref, order_ref, x_ref, field_ref, edge_ref, levs,
+    lat_ref, col_ref, recv_ref, order_ref, lon_ref, tilt_ref, table_hi_ref, table_lo_ref, twiddle_ref,
+    grid_ref, departed_ref, x_ref, field_ref, edge_ref, lat_smem, col_smem, lat_sem, col_sem, levs,
 ):
+    lat_copy = pltpu.make_async_copy(lat_ref, lat_smem, lat_sem)
+    lat_copy.start()
+    col_copy = pltpu.make_async_copy(col_ref, col_smem, col_sem)
+    col_copy.start()
     wave = lax.axis_index("wave")
     last = lax.axis_index("lev") == levs - 1
-    top = 640
-    order_into(order_ref, low_ref, top)
 
     lane = lax.broadcasted_iota(jnp.int32, (8, 128), 1)
     slot = lane // 16
@@ -319,6 +341,8 @@
                 lev, h = row // 2, row % 2
                 grid_ref[lev, pl.ds(2 * h + l, 1), pl.ds(128 * x, 128)] = field_ref[x, pl.ds(8 * (2 + l) + row, 1), :]
 
+    lat_copy.wait()
+    col_copy.wait()
     hemi = lax.broadcasted_iota(jnp.int32, (8, 128), 0) % 2 == 1
     keep_own = jnp.logical_and(last, lax.broadcasted_iota(jnp.int32, (8, 128), 0) >= 2)
     for l in range(2):
@@ -335,7 +359,7 @@
             lon, tilt = pick(lon_ref), pick(tilt_ref)
 
             def shift_of(block):
-                return lax.rem(col_ref[block] - 128 * x + 1280 + 640, 1280) - 640
+                return lax.rem(col_smem[block] - 128 * x + 1280 + 640, 1280) - 640
 
             base = jnp.where(hemi, shift_of(south), shift_of(north))
             index = lane + base + (lon >> 2) - 3
@@ -346,7 +370,7 @@
             rows = []
             for off in range(2):
                 starts = [
-                    pl.multiple_of(8 * (lat_ref[block] - 2 * wave + 2 + off), 8) for block in (north, south)
+                    pl.multiple_of(8 * (lat_smem[block] - 2 * wave + 2 + off), 8) for block in (north, south)
                 ]
                 main = jnp.where(hemi, field_ref[x, pl.ds(starts[1], 8), :], field_ref[x, pl.ds(starts[0], 8), :])
                 edge = jnp.where(hemi, edge_ref[x, pl.ds(starts[1], 8), :], edge_ref[x, pl.ds(starts[0], 8), :])
@@ -384,34 +408,38 @@
     return hi, lo, twiddle
 
 
-def to_grid(pair_low, dep_lat, dep_col, received, lon_steps, tilt_steps, levs):
+def to_grid(dep_lat, dep_col, received, order, lon_steps, tilt_steps, levs):
     hi, lo, twiddle = dft_tables()
     vmem = pl.BlockSpec(memory_space=pltpu.VMEM)
-    smem = pl.BlockSpec(memory_space=pltpu.SMEM)
+    outside = pl.BlockSpec(memory_space=pl.ANY)
 
     def kernel(*refs):
         grid_kernel(*refs, levs)
 
-    low = jnp.pad(pair_low, (0, 64), constant_values=-1)
     return pl.pallas_call(
         kernel,
         out_shape=[jax.ShapeDtypeStruct((2, 4, 1280), f32)] * 2,
-        in_specs=[vmem, smem, smem] + [vmem] * 6,
+        in_specs=[outside, outside] + [vmem] * 7,
         out_specs=[vmem, vmem],
         scratch_shapes=[
-            pltpu.VMEM((2, 384, 512), bf16),
             pltpu.VMEM((2, 192, 512), bf16),
             pltpu.VMEM((10, 48, 128), f32),
             pltpu.VMEM((10, 48, 128), f32),
+            pltpu.SMEM(dep_lat.shape, jnp.int32),
+            pltpu.SMEM(dep_col.shape, jnp.int32),
+            pltpu.SemaphoreType.DMA,
+            pltpu.SemaphoreType.DMA,
         ],
+        compiler_params=pltpu.CompilerParams(vmem_limit_bytes=LIMIT),
         name="grid",
-    )(low, dep_lat, dep_col, received, lon_steps, tilt_steps, jnp.asarray(hi), jnp.asarray(lo), jnp.asarray(twiddle))
+    )(dep_lat, dep_col, received, order, lon_steps, tilt_steps, jnp.asarray(hi), jnp.asarray(lo), jnp.asarray(twiddle))
 
 
 def per_device(legendre, spectral, pair_low, dep_lat, dep_col, lon_steps, tilt_steps):
     waves, levs = lax.axis_size("wave"), lax.axis_size("lev")
-    received = exchange(pair_low, legendre, spectral, waves, levs).reshape(waves, 3, 8, 128)
-    return tuple(to_grid(pair_low, dep_lat, dep_col, received, lon_steps, tilt_steps, levs))
+    received, order = exchange(pair_low, legendre, spectral, waves, levs)
+    received = received.reshape(waves, 3, 8, 128)
+    return tuple(to_grid(dep_lat, dep_col, received, order, lon_steps, tilt_steps, levs))
 
 
 def solution(mesh):

time: 37.2 us -> 28.1 us (0.76)
  Pallas kernels: 35 us -> 27.2 us
  local copies, waits for them, and re-layouts: 1.26 us -> 0.04 us
    pallas_call x1, Pallas kernels: 31.8 us -> 24.9 us  [exchange(): pl.pallas_call(functools.partial(exchange_kernel, waves, levs), out_shape...]
    pad x1 -> x0, local copies, waits for them, and re-layouts: 1.26 us -> none  [to_grid(): low = jnp.pad(pair_low, (0, 64), constant_values=-1)]
    pallas_call x1, Pallas kernels: 3.23 us -> 2.3 us  [to_grid(): pl.pallas_call(kernel, out_shape=[jax.ShapeDtypeStruct((2, 4, 1280), f32)...]
where the time goes in v2:
time: 28.1 us; the launch traced here: 28 us
  Pallas kernels  27.2 us (97%)
  between operations  0.75 us (3%)
    pallas_call x1, Pallas kernels, exchange(): pl.pallas_call(functools.partial(exchange_kernel, waves, levs), out_shape...  24.9 us
    pallas_call x1, Pallas kernels, to_grid(): pl.pallas_call(kernel, out_shape=[jax.ShapeDtypeStruct((2, 4, 1280), f32)...  2.3 us

profile of v2, /device:TPU:1, one launch (start us, length us, event | category | flops | bytes accessed | tf_op | source)
XLA Modules:
  0.0 28.0 jit_solution(11385828745576965876)
XLA Ops:
  0.6 0.0 copy-start.4
  0.6 0.0 copy-start
  0.7 0.0 copy-start.1
  0.7 0.0 copy-start.3
  0.7 0.0 copy-start.2
  0.7 0.0 copy-start.6
  0.7 0.0 copy-start.5
  0.7 24.9 %shard_map.113 = (f32[32,3,4,2,128]{4,3,2,1,0:T(2,128)S(1)}, bf16[2,384,512]{2,1,0:T(8,128)(2,1)S(1)}) custom-call(s32[320]{0:T(512)} %low_hbm.1, f32[10,64,641]{2,1,0:T(8,128)} %leg_hbm.1, f32[10,2,2,641]{3,2,1,0:T(2,128)} %spec_hbm.1), custom_call_target="tpu_custom_call" | custom-call | tf_op jit(solution)/shard_map/pallas_call | solution.py:169
  25.6 0.0 copy-done.4
  25.6 0.0 copy-done
  25.6 0.0 copy-done.1
  25.6 0.0 copy-done.3
  25.6 0.0 copy-done.2
  25.7 0.0 copy-done.6
  25.7 0.0 copy-done.5
  25.7 2.3 %grid.1 = (f32[2,4,1280]{2,1,0:T(4,128)}, f32[2,4,1280]{2,1,0:T(4,128)}) custom-call(s32[40]{0:T(128)S(1)} %copy-done.5, s32[40]{0:T(128)S(1)} %copy-done.6, f32[32,3,8,128]{3,2,1,0:T(8,128)S(1)} %bitcast.1, bf16[2,384,512]{2,1,0:T(8,128)(2,1)S(1)} %get-tuple-element.5.refs_3_, s32[40,128]{1,0:T(8,128)S(1)} %copy-done.2, s32[40,128]{1,0:T(8,128)S(1)} %copy-done.3, ...), custom_call_target="tpu_custom_call" | custom-call | tf_op jit(solution)/shard_map/grid/pallas_call | solution.py:419
Async XLA Ops:
  0.6 25.0 %copy-start.4 = (f32[20,128]{1,0:T(8,128)S(1)}, f32[20,128]{1,0:T(8,128)}, u32[]{:S(2)}) copy-start(f32[20,128]{1,0:T(8,128)} %constant.8.clone.refs_8_) | copy-start | bytes 30724
  0.6 25.0 %copy-start = (bf16[224,256]{1,0:T(8,128)(2,1)S(1)}, bf16[224,256]{1,0:T(8,128)(2,1)}, u32[]{:S(2)}) copy-start(bf16[224,256]{1,0:T(8,128)(2,1)} %constant.7.clone.refs_7_) | copy-start | bytes 344068
  0.7 25.0 %copy-start.1 = (bf16[224,256]{1,0:T(8,128)(2,1)S(1)}, bf16[224,256]{1,0:T(8,128)(2,1)}, u32[]{:S(2)}) copy-start(bf16[224,256]{1,0:T(8,128)(2,1)} %constant.6.clone.refs_6_) | copy-start | bytes 344068
  0.7 25.0 %copy-start.3 = (s32[40,128]{1,0:T(8,128)S(1)}, s32[40,128]{1,0:T(8,128)}, u32[]{:S(2)}) copy-start(s32[40,128]{1,0:T(8,128)} %refs_5_.1) | copy-start | bytes 61444
  0.7 25.0 %copy-start.2 = (s32[40,128]{1,0:T(8,128)S(1)}, s32[40,128]{1,0:T(8,128)}, u32[]{:S(2)}) copy-start(s32[40,128]{1,0:T(8,128)} %refs_4_.1) | copy-start | bytes 61444
  0.7 25.0 %copy-start.6 = (s32[40]{0:T(128)S(1)}, s32[40]{0:T(128)}, u32[]{:S(2)}) copy-start(s32[40]{0:T(128)} %refs_1_.1) | copy-start | bytes 484
  0.7 25.0 %copy-start.5 = (s32[40]{0:T(128)S(1)}, s32[40]{0:T(128)}, u32[]{:S(2)}) copy-start(s32[40]{0:T(128)} %refs_0_.1) | copy-start | bytes 484

commit v3 on v2

--- a/solution.py
+++ b/solution.py
@@ -65,7 +65,7 @@
 def exchange_kernel(
     waves, levs, low_hbm, leg_hbm, spec_hbm, recv_ref, order_ref,
     low_smem, low_vmem, leg_ref, spec_ref, y_ref, z_ref, send_ref,
-    low_sem, leg_sem, spec_sem, send_sem, recv_sem, down_send_sem, down_recv_sem,
+    low_sem, leg_sem, spec_sem, send_sem, recv_sem, down_send_sem, down_recv_sem, ready, ready_down,
 ):
     me = lax.axis_index("wave")
     lev = lax.axis_index("lev")
@@ -83,20 +83,40 @@
     low_again.start()
 
     barrier = pltpu.get_barrier_semaphore()
-
-    def greet(d, _):
-        pl.semaphore_signal(barrier, inc=1, device_id={"lev": lev, "wave": lax.rem(me + d, waves)}, device_id_type=MESH)
-        return 0
-
-    def greet_above(w, _):
-        pl.semaphore_signal(barrier, inc=1, device_id={"lev": lev + 1, "wave": w}, device_id_type=MESH)
-        return 0
-
-    lax.fori_loop(1, waves, greet, 0)
-
-    @pl.when(lev < levs - 1)
-    def _():
-        lax.fori_loop(0, waves, greet_above, 0)
+    late = me == 0
+    lower, upper = lev > 0, lev < levs - 1
+    peers, all_waves = waves - 1, waves
+
+    def signal(sem, to_lev, to_wave):
+        pl.semaphore_signal(sem, inc=1, device_id={"lev": to_lev, "wave": to_wave}, device_id_type=MESH)
+
+    def each(first, body):
+        def step(d, _):
+            body(d)
+            return 0
+
+        lax.fori_loop(first, waves, step, 0)
+
+    @pl.when(jnp.logical_not(late))
+    def _():
+        each(1, lambda d: signal(barrier, lev, lax.rem(me + d, waves)))
+
+        @pl.when(upper)
+        def _():
+            each(0, lambda w: signal(barrier, lev + 1, w))
+
+    @pl.when(lower)
+    def _():
+        signal(barrier, lev - 1, 0)
+
+    @pl.when(late)
+    def _():
+        pl.semaphore_wait(barrier, peers + jnp.where(lower, peers, 0) + jnp.where(upper, all_waves, 0))
+        each(1, lambda d: signal(ready, lev, d))
+
+        @pl.when(upper)
+        def _():
+            each(0, lambda w: signal(ready_down, lev + 1, w))
 
     low_copy.wait()
 
@@ -109,10 +129,12 @@
         send_ref, lambda s: low_smem[me * pairs + s], leg_ref, spec_ref, wait_pair, y_ref, z_ref,
         lax.rem(me, 8),
     )
-    pl.semaphore_wait(barrier, waves - 1 + jnp.where(lev > 0, waves, 0))
-
-    def across(d, _):
-        peer = lax.rem(me + d, waves)
+
+    @pl.when(jnp.logical_not(late))
+    def _():
+        pl.semaphore_wait(barrier, peers - 1 + jnp.where(lower, peers, 0))
+
+    def across(peer):
         pltpu.make_async_remote_copy(
             src_ref=send_ref.at[pl.ds(peer, 3)],
             dst_ref=recv_ref.at[me, :, pl.ds(0, 2)],
@@ -121,10 +143,8 @@
             device_id={"lev": lev, "wave": peer},
             device_id_type=MESH,
         ).start()
-        return 0
-
-    def down(d, _):
-        peer = lax.rem(me + d, waves)
+
+    def down(peer):
         pltpu.make_async_remote_copy(
             src_ref=send_ref.at[pl.ds(peer, 3), 0],
             dst_ref=recv_ref.at[me, :, 2],
@@ -133,31 +153,47 @@
             device_id={"lev": lev - 1, "wave": peer},
             device_id_type=MESH,
         ).start()
-        return 0
-
-    lax.fori_loop(1, waves, across, 0)
-
-    @pl.when(lev > 0)
-    def _():
-        lax.fori_loop(0, waves, down, 0)
+
+    def spread(d):
+        peer = lax.rem(me + d, waves)
+
+        @pl.when(peer != 0)
+        def _():
+            across(peer)
+
+    each(1, spread)
+
+    @pl.when(lower)
+    def _():
+        each(1, down)
 
     own = pltpu.make_async_copy(send_ref.at[pl.ds(me, 3)], recv_ref.at[me, :, pl.ds(0, 2)], recv_sem)
     own.start()
     low_again.wait()
     order_into(order_ref, low_vmem, slots - 1)
 
+    @pl.when(jnp.logical_not(late))
+    def _():
+        pl.semaphore_wait(ready, 1)
+        across(0)
+
+    @pl.when(lower)
+    def _():
+        pl.semaphore_wait(ready_down, 1)
+        down(0)
+
     all_across = recv_ref.at[:, :, pl.ds(0, 2)]
     sent_across = recv_ref.at[pl.ds(0, waves - 1), :, pl.ds(0, 2)]
     all_down = recv_ref.at[:, :, 2]
     pltpu.make_async_copy(all_across, all_across, recv_sem).wait()
 
-    @pl.when(lev < levs - 1)
+    @pl.when(upper)
     def _():
         pltpu.make_async_copy(all_down, all_down, down_recv_sem).wait()
 
     pltpu.make_async_copy(sent_across, sent_across, send_sem).wait()
 
-    @pl.when(lev > 0)
+    @pl.when(lower)
     def _():
         pltpu.make_async_copy(all_down, all_down, down_send_sem).wait()
 
@@ -189,6 +225,8 @@
             pltpu.SemaphoreType.DMA,
             pltpu.SemaphoreType.DMA,
             pltpu.SemaphoreType.DMA,
+            pltpu.SemaphoreType.REGULAR,
+            pltpu.SemaphoreType.REGULAR,
         ],
         compiler_params=pltpu.CompilerParams(
             collective_id=0, has_side_effects=True, vmem_limit_bytes=LIMIT

time: 28.1 us -> 24 us (0.85)
  the two profiles are of different devices: /device:TPU:1 before, /device:TPU:29 now
where the time goes in v3:
time: 24 us; the launch traced here: 23.8 us
  Pallas kernels  23.1 us (96%)
  between operations  0.75 us (3%)
    pallas_call x1, Pallas kernels, exchange(): pl.pallas_call(functools.partial(exchange_kernel, waves, levs), out_shape...  20.8 us
    pallas_call x1, Pallas kernels, to_grid(): pl.pallas_call(kernel, out_shape=[jax.ShapeDtypeStruct((2, 4, 1280), f32)...  2.31 us

profile of v3, /device:TPU:29, one launch (start us, length us, event | category | flops | bytes accessed | tf_op | source)
XLA Modules:
  0.0 23.8 jit_solution(6637897079250985601)
XLA Ops:
  0.6 0.0 copy-start.4
  0.6 0.0 copy-start
  0.7 0.0 copy-start.1
  0.7 0.0 copy-start.3
  0.7 0.0 copy-start.2
  0.7 0.0 copy-start.6
  0.7 0.0 copy-start.5
  0.7 20.8 %shard_map.113 = (f32[32,3,4,2,128]{4,3,2,1,0:T(2,128)S(1)}, bf16[2,384,512]{2,1,0:T(8,128)(2,1)S(1)}) custom-call(s32[320]{0:T(512)} %low_hbm.1, f32[10,64,641]{2,1,0:T(8,128)} %leg_hbm.1, f32[10,2,2,641]{3,2,1,0:T(2,128)} %spec_hbm.1), custom_call_target="tpu_custom_call" | custom-call | tf_op jit(solution)/shard_map/pallas_call | solution.py:205
  21.5 0.0 copy-done.4
  21.5 0.0 copy-done
  21.5 0.0 copy-done.1
  21.5 0.0 copy-done.3
  21.5 0.0 copy-done.2
  21.5 0.0 copy-done.6
  21.5 0.0 copy-done.5
  21.5 2.3 %grid.1 = (f32[2,4,1280]{2,1,0:T(4,128)}, f32[2,4,1280]{2,1,0:T(4,128)}) custom-call(s32[40]{0:T(128)S(1)} %copy-done.5, s32[40]{0:T(128)S(1)} %copy-done.6, f32[32,3,8,128]{3,2,1,0:T(8,128)S(1)} %bitcast.1, bf16[2,384,512]{2,1,0:T(8,128)(2,1)S(1)} %get-tuple-element.5.refs_3_, s32[40,128]{1,0:T(8,128)S(1)} %copy-done.2, s32[40,128]{1,0:T(8,128)S(1)} %copy-done.3, ...), custom_call_target="tpu_custom_call" | custom-call | tf_op jit(solution)/shard_map/grid/pallas_call | solution.py:457
Async XLA Ops:
  0.6 20.8 %copy-start.4 = (f32[20,128]{1,0:T(8,128)S(1)}, f32[20,128]{1,0:T(8,128)}, u32[]{:S(2)}) copy-start(f32[20,128]{1,0:T(8,128)} %constant.8.clone.refs_8_) | copy-start | bytes 30724
  0.6 20.8 %copy-start = (bf16[224,256]{1,0:T(8,128)(2,1)S(1)}, bf16[224,256]{1,0:T(8,128)(2,1)}, u32[]{:S(2)}) copy-start(bf16[224,256]{1,0:T(8,128)(2,1)} %constant.7.clone.refs_7_) | copy-start | bytes 344068
  0.7 20.8 %copy-start.1 = (bf16[224,256]{1,0:T(8,128)(2,1)S(1)}, bf16[224,256]{1,0:T(8,128)(2,1)}, u32[]{:S(2)}) copy-start(bf16[224,256]{1,0:T(8,128)(2,1)} %constant.6.clone.refs_6_) | copy-start | bytes 344068
  0.7 20.8 %copy-start.3 = (s32[40,128]{1,0:T(8,128)S(1)}, s32[40,128]{1,0:T(8,128)}, u32[]{:S(2)}) copy-start(s32[40,128]{1,0:T(8,128)} %refs_5_.1) | copy-start | bytes 61444
  0.7 20.8 %copy-start.2 = (s32[40,128]{1,0:T(8,128)S(1)}, s32[40,128]{1,0:T(8,128)}, u32[]{:S(2)}) copy-start(s32[40,128]{1,0:T(8,128)} %refs_4_.1) | copy-start | bytes 61444
  0.7 20.8 %copy-start.6 = (s32[40]{0:T(128)S(1)}, s32[40]{0:T(128)}, u32[]{:S(2)}) copy-start(s32[40]{0:T(128)} %refs_1_.1) | copy-start | bytes 484
  0.7 20.8 %copy-start.5 = (s32[40]{0:T(128)S(1)}, s32[40]{0:T(128)}, u32[]{:S(2)}) copy-start(s32[40]{0:T(128)} %refs_0_.1) | copy-start | bytes 484

commit v4 on v3

--- a/solution.py
+++ b/solution.py
@@ -65,7 +65,8 @@
 def exchange_kernel(
     waves, levs, low_hbm, leg_hbm, spec_hbm, recv_ref, order_ref,
     low_smem, low_vmem, leg_ref, spec_ref, y_ref, z_ref, send_ref,
-    low_sem, leg_sem, spec_sem, send_sem, recv_sem, down_send_sem, down_recv_sem, ready, ready_down,
+    low_sem, leg_sem, spec_sem, send_sem, recv_sem, down_send_sem, down_recv_sem,
+    proxy_ref, proxy_sem, proxy_down_sem, relay_sem, relay_down_sem, ready,
 ):
     me = lax.axis_index("wave")
     lev = lax.axis_index("lev")
@@ -85,7 +86,7 @@
     barrier = pltpu.get_barrier_semaphore()
     late = me == 0
     lower, upper = lev > 0, lev < levs - 1
-    peers, all_waves = waves - 1, waves
+    peers = waves - 1
 
     def signal(sem, to_lev, to_wave):
         pl.semaphore_signal(sem, inc=1, device_id={"lev": to_lev, "wave": to_wave}, device_id_type=MESH)
@@ -105,25 +106,18 @@
         def _():
             each(0, lambda w: signal(barrier, lev + 1, w))
 
-    @pl.when(lower)
-    def _():
-        signal(barrier, lev - 1, 0)
-
     @pl.when(late)
     def _():
-        pl.semaphore_wait(barrier, peers + jnp.where(lower, peers, 0) + jnp.where(upper, all_waves, 0))
-        each(1, lambda d: signal(ready, lev, d))
-
-        @pl.when(upper)
-        def _():
-            each(0, lambda w: signal(ready_down, lev + 1, w))
+        pl.semaphore_wait(barrier, peers + jnp.where(lower, peers, 0))
+        signal(ready, lev, 1)
 
     low_copy.wait()
 
     def wait_pair(s):
         if s == 0:
             spec_copy.wait()
-        leg_copies[s].wait()
+            for copy in leg_copies:
+                copy.wait()
 
     legendre_into(
         send_ref, lambda s: low_smem[me * pairs + s], leg_ref, spec_ref, wait_pair, y_ref, z_ref,
@@ -134,68 +128,105 @@
     def _():
         pl.semaphore_wait(barrier, peers - 1 + jnp.where(lower, peers, 0))
 
-    def across(peer):
+    def across(peer, slots_of, to_wave, sem):
         pltpu.make_async_remote_copy(
             src_ref=send_ref.at[pl.ds(peer, 3)],
-            dst_ref=recv_ref.at[me, :, pl.ds(0, 2)],
+            dst_ref=slots_of.at[me, :, pl.ds(0, 2)],
             send_sem=send_sem,
-            recv_sem=recv_sem,
-            device_id={"lev": lev, "wave": peer},
+            recv_sem=sem,
+            device_id={"lev": lev, "wave": to_wave},
             device_id_type=MESH,
         ).start()
 
-    def down(peer):
+    def down(peer, slots_of, to_wave, sem):
         pltpu.make_async_remote_copy(
             src_ref=send_ref.at[pl.ds(peer, 3), 0],
-            dst_ref=recv_ref.at[me, :, 2],
+            dst_ref=slots_of.at[me, :, 2],
             send_sem=down_send_sem,
-            recv_sem=down_recv_sem,
-            device_id={"lev": lev - 1, "wave": peer},
+            recv_sem=sem,
+            device_id={"lev": lev - 1, "wave": to_wave},
             device_id_type=MESH,
         ).start()
 
     def spread(d):
-        peer = lax.rem(me + d, waves)
-
-        @pl.when(peer != 0)
+        peer = lax.rem(me + waves // 2 + d, waves)
+
+        @pl.when(jnp.logical_and(peer != 0, peer != me))
         def _():
-            across(peer)
-
-    each(1, spread)
+            across(peer, recv_ref, peer, recv_sem)
+
+    each(0, spread)
+
+    @pl.when(me > 1)
+    def _():
+        across(0, proxy_ref, 1, proxy_sem)
 
     @pl.when(lower)
     def _():
-        each(1, down)
-
-    own = pltpu.make_async_copy(send_ref.at[pl.ds(me, 3)], recv_ref.at[me, :, pl.ds(0, 2)], recv_sem)
-    own.start()
+        each(1, lambda w: down(w, recv_ref, w, down_recv_sem))
+        down(0, proxy_ref, 1, proxy_down_sem)
+
+    pltpu.make_async_copy(send_ref.at[pl.ds(me, 3)], recv_ref.at[me, :, pl.ds(0, 2)], recv_sem).start()
     low_again.wait()
     order_into(order_ref, low_vmem, slots - 1)
 
-    @pl.when(jnp.logical_not(late))
-    def _():
+    def wait_for(part, sem):
+        pltpu.make_async_copy(part, part, sem).wait()
+
+    def relay(part_of, sem, to_sem):
+        return pltpu.make_async_remote_copy(
+            src_ref=part_of(proxy_ref),
+            dst_ref=part_of(recv_ref),
+            send_sem=sem,
+            recv_sem=to_sem,
+            device_id={"lev": lev, "wave": 0},
+            device_id_type=MESH,
+        )
+
+    def others(ref):
+        return ref.at[pl.ds(1, waves - 1), :, pl.ds(0, 2)]
+
+    def downs(ref):
+        return ref.at[:, :, 2]
+
+    @pl.when(me == 1)
+    def _():
+        pltpu.make_async_copy(send_ref.at[pl.ds(0, 3)], proxy_ref.at[me, :, pl.ds(0, 2)], proxy_sem).start()
+        wait_for(others(proxy_ref), proxy_sem)
+
+        @pl.when(upper)
+        def _():
+            wait_for(downs(proxy_ref), proxy_down_sem)
+
         pl.semaphore_wait(ready, 1)
-        across(0)
+        relay(others, relay_sem, recv_sem).start()
+
+        @pl.when(upper)
+        def _():
+            relay(downs, relay_down_sem, down_recv_sem).start()
+
+    wait_for(recv_ref.at[:, :, pl.ds(0, 2)], recv_sem)
+
+    @pl.when(upper)
+    def _():
+        wait_for(downs(recv_ref), down_recv_sem)
+
+    @pl.when(me == 1)
+    def _():
+        wait_for(others(proxy_ref), relay_sem)
+        wait_for(recv_ref.at[pl.ds(0, waves - 2), :, pl.ds(0, 2)], send_sem)
+
+        @pl.when(upper)
+        def _():
+            wait_for(downs(proxy_ref), relay_down_sem)
+
+    @pl.when(me != 1)
+    def _():
+        wait_for(others(recv_ref), send_sem)
 
     @pl.when(lower)
     def _():
-        pl.semaphore_wait(ready_down, 1)
-        down(0)
-
-    all_across = recv_ref.at[:, :, pl.ds(0, 2)]
-    sent_across = recv_ref.at[pl.ds(0, waves - 1), :, pl.ds(0, 2)]
-    all_down = recv_ref.at[:, :, 2]
-    pltpu.make_async_copy(all_across, all_across, recv_sem).wait()
-
-    @pl.when(upper)
-    def _():
-        pltpu.make_async_copy(all_down, all_down, down_recv_sem).wait()
-
-    pltpu.make_async_copy(sent_across, sent_across, send_sem).wait()
-
-    @pl.when(lower)
-    def _():
-        pltpu.make_async_copy(all_down, all_down, down_send_sem).wait()
+        wait_for(downs(recv_ref), down_send_sem)
 
 
 def exchange(pair_low, legendre, spectral, waves, levs):
@@ -225,7 +256,11 @@
             pltpu.SemaphoreType.DMA,
             pltpu.SemaphoreType.DMA,
             pltpu.SemaphoreType.DMA,
-            pltpu.SemaphoreType.REGULAR,
+            pltpu.VMEM((waves, 3, 4, 2, 128), f32),
+            pltpu.SemaphoreType.DMA,
+            pltpu.SemaphoreType.DMA,
+            pltpu.SemaphoreType.DMA,
+            pltpu.SemaphoreType.DMA,
             pltpu.SemaphoreType.REGULAR,
         ],
         compiler_params=pltpu.CompilerParams(

time: 24 us -> 22.4 us (0.933)
  the two profiles are of different devices: /device:TPU:29 before, /device:TPU:27 now
where the time goes in v4:
time: 22.4 us; the launch traced here: 22.3 us
  Pallas kernels  21.5 us (96%)
  between operations  0.75 us (3%)
    pallas_call x1, Pallas kernels, exchange(): pl.pallas_call(functools.partial(exchange_kernel, waves, levs), out_shape...  19.2 us
    pallas_call x1, Pallas kernels, to_grid(): pl.pallas_call(kernel, out_shape=[jax.ShapeDtypeStruct((2, 4, 1280), f32)...  2.29 us

profile of v4, /device:TPU:27, one launch (start us, length us, event | category | flops | bytes accessed | tf_op | source)
XLA Modules:
  0.0 22.3 jit_solution(18180776810455223534)
XLA Ops:
  0.6 0.0 copy-start.4
  0.6 0.0 copy-start
  0.7 0.0 copy-start.1
  0.7 0.0 copy-start.3
  0.7 0.0 copy-start.2
  0.7 0.0 copy-start.6
  0.7 0.0 copy-start.5
  0.7 19.2 %shard_map.113 = (f32[32,3,4,2,128]{4,3,2,1,0:T(2,128)S(1)}, bf16[2,384,512]{2,1,0:T(8,128)(2,1)S(1)}) custom-call(s32[320]{0:T(512)} %low_hbm.1, f32[10,64,641]{2,1,0:T(8,128)} %leg_hbm.1, f32[10,2,2,641]{3,2,1,0:T(2,128)} %spec_hbm.1), custom_call_target="tpu_custom_call" | custom-call | tf_op jit(solution)/shard_map/pallas_call | solution.py:236
  19.9 0.0 copy-done.4
  19.9 0.0 copy-done
  19.9 0.0 copy-done.1
  19.9 0.0 copy-done.3
  19.9 0.0 copy-done.2
  20.0 0.0 copy-done.6
  20.0 0.0 copy-done.5
  20.0 2.3 %grid.1 = (f32[2,4,1280]{2,1,0:T(4,128)}, f32[2,4,1280]{2,1,0:T(4,128)}) custom-call(s32[40]{0:T(128)S(1)} %copy-done.5, s32[40]{0:T(128)S(1)} %copy-done.6, f32[32,3,8,128]{3,2,1,0:T(8,128)S(1)} %bitcast.1, bf16[2,384,512]{2,1,0:T(8,128)(2,1)S(1)} %get-tuple-element.5.refs_3_, s32[40,128]{1,0:T(8,128)S(1)} %copy-done.2, s32[40,128]{1,0:T(8,128)S(1)} %copy-done.3, ...), custom_call_target="tpu_custom_call" | custom-call | tf_op jit(solution)/shard_map/grid/pallas_call | solution.py:492
Async XLA Ops:
  0.6 19.3 %copy-start.4 = (f32[20,128]{1,0:T(8,128)S(1)}, f32[20,128]{1,0:T(8,128)}, u32[]{:S(2)}) copy-start(f32[20,128]{1,0:T(8,128)} %constant.8.clone.refs_8_) | copy-start | bytes 30724
  0.6 19.3 %copy-start = (bf16[224,256]{1,0:T(8,128)(2,1)S(1)}, bf16[224,256]{1,0:T(8,128)(2,1)}, u32[]{:S(2)}) copy-start(bf16[224,256]{1,0:T(8,128)(2,1)} %constant.7.clone.refs_7_) | copy-start | bytes 344068
  0.7 19.3 %copy-start.1 = (bf16[224,256]{1,0:T(8,128)(2,1)S(1)}, bf16[224,256]{1,0:T(8,128)(2,1)}, u32[]{:S(2)}) copy-start(bf16[224,256]{1,0:T(8,128)(2,1)} %constant.6.clone.refs_6_) | copy-start | bytes 344068
  0.7 19.3 %copy-start.3 = (s32[40,128]{1,0:T(8,128)S(1)}, s32[40,128]{1,0:T(8,128)}, u32[]{:S(2)}) copy-start(s32[40,128]{1,0:T(8,128)} %refs_5_.1) | copy-start | bytes 61444
  0.7 19.3 %copy-start.2 = (s32[40,128]{1,0:T(8,128)S(1)}, s32[40,128]{1,0:T(8,128)}, u32[]{:S(2)}) copy-start(s32[40,128]{1,0:T(8,128)} %refs_4_.1) | copy-start | bytes 61444
  0.7 19.3 %copy-start.6 = (s32[40]{0:T(128)S(1)}, s32[40]{0:T(128)}, u32[]{:S(2)}) copy-start(s32[40]{0:T(128)} %refs_1_.1) | copy-start | bytes 484
  0.7 19.3 %copy-start.5 = (s32[40]{0:T(128)S(1)}, s32[40]{0:T(128)}, u32[]{:S(2)}) copy-start(s32[40]{0:T(128)} %refs_0_.1) | copy-start | bytes 484

commit v5 on v4

--- a/solution.py
+++ b/solution.py
@@ -27,21 +27,27 @@
     top = slots - 1
     k = lax.broadcasted_iota(jnp.int32, (8, slots), 1)
     row = lax.broadcasted_iota(jnp.int32, (8, slots), 0)
-    hemi, member, part = row // 4, (row // 2) % 2, row % 2
+    southern, second, real = row >= 4, (row & 2) != 0, (row & 1) == 0
+    signed_k = jnp.where(second, k, -k)
+
+    def signs(parity):
+        return jnp.where(jnp.logical_and(southern, parity != 0), -1.0, 1.0)
+
+    sign_even = signs(k & 1)
+    sign_odd = jnp.where(second, signs((k + 1) & 1), sign_even)
     y_ref[...] = jnp.zeros_like(y_ref)
     send_ref[0] = jnp.zeros(send_ref.shape[1:], f32)
     send_ref[lats // 2 + 1] = jnp.zeros(send_ref.shape[1:], f32)
     for s in range(pairs):
         wait_pair(s)
         first = top - low_of(s)
-        keep = (k >= first) == (member == 1)
-        odd = (k + member * first) % 2
-        mask = jnp.where(keep, 1 - 2 * (hemi * odd), 0).astype(f32)
+        keep = signed_k >= jnp.where(second, first, 1 - first)
+        mask = jnp.where(keep, jnp.where((first & 1) == 0, sign_even, sign_odd), 0.0)
         rows = []
         for lev in range(2):
             re = jnp.broadcast_to(spec_ref[s, lev, 0:1, :], (8, slots))
             im = jnp.broadcast_to(spec_ref[s, lev, 1:2, :], (8, slots))
-            rows.append(jnp.where(part == 0, re, im) * mask)
+            rows.append(jnp.where(real, re, im) * mask)
         hi, lo = split(jnp.concatenate(rows, axis=0))
         leg_hi, leg_lo = split(leg_ref[s])
         both = lax.dot_general(jnp.concatenate([hi, lo], axis=0), leg_hi, NT, preferred_element_type=f32)
@@ -63,10 +69,12 @@
 
 
 def exchange_kernel(
-    waves, levs, low_hbm, leg_hbm, spec_hbm, recv_ref, order_ref,
+    waves, levs, low_hbm, leg_hbm, spec_hbm, col_hbm, lon_hbm, tilt_hbm,
+    recv_ref, order_ref, index_ref, mix_ref,
     low_smem, low_vmem, leg_ref, spec_ref, y_ref, z_ref, send_ref,
     low_sem, leg_sem, spec_sem, send_sem, recv_sem, down_send_sem, down_recv_sem,
     proxy_ref, proxy_sem, proxy_down_sem, relay_sem, relay_down_sem, ready,
+    col_smem, lon_vmem, tilt_vmem, plan_sem,
 ):
     me = lax.axis_index("wave")
     lev = lax.axis_index("lev")
@@ -82,6 +90,12 @@
         copy.start()
     low_again = pltpu.make_async_copy(low_hbm, low_vmem, low_sem.at[1])
     low_again.start()
+    plan_copies = [
+        pltpu.make_async_copy(src, dst, plan_sem.at[i])
+        for i, (src, dst) in enumerate([(col_hbm, col_smem), (lon_hbm, lon_vmem), (tilt_hbm, tilt_vmem)])
+    ]
+    for copy in plan_copies:
+        copy.start()
 
     barrier = pltpu.get_barrier_semaphore()
     late = me == 0
@@ -169,6 +183,9 @@
     pltpu.make_async_copy(send_ref.at[pl.ds(me, 3)], recv_ref.at[me, :, pl.ds(0, 2)], recv_sem).start()
     low_again.wait()
     order_into(order_ref, low_vmem, slots - 1)
+    for copy in plan_copies:
+        copy.wait()
+    plan_into(index_ref, mix_ref, col_smem, lon_vmem, tilt_vmem)
 
     def wait_for(part, sem):
         pltpu.make_async_copy(part, part, sem).wait()
@@ -229,18 +246,21 @@
         wait_for(downs(recv_ref), down_send_sem)
 
 
-def exchange(pair_low, legendre, spectral, waves, levs):
+def exchange(pair_low, legendre, spectral, dep_col, lon_steps, tilt_steps, waves, levs):
     pairs, lats, slots = legendre.shape
     any_space = pl.BlockSpec(memory_space=pltpu.HBM)
+    operands = (pair_low, legendre, spectral, dep_col, lon_steps, tilt_steps)
     vmem = pl.BlockSpec(memory_space=pltpu.VMEM)
     return pl.pallas_call(
         functools.partial(exchange_kernel, waves, levs),
         out_shape=[
             jax.ShapeDtypeStruct((waves, 3, 4, 2, 128), f32),
             jax.ShapeDtypeStruct((2, 384, 512), bf16),
+            jax.ShapeDtypeStruct((20, 8, 128), jnp.int32),
+            jax.ShapeDtypeStruct((20, 5, 8, 128), f32),
         ],
-        in_specs=[any_space] * 3,
-        out_specs=[vmem, vmem],
+        in_specs=[any_space] * 6,
+        out_specs=[vmem] * 4,
         scratch_shapes=[
             pltpu.SMEM(pair_low.shape, jnp.int32),
             pltpu.VMEM(pair_low.shape, jnp.int32),
@@ -262,11 +282,15 @@
             pltpu.SemaphoreType.DMA,
             pltpu.SemaphoreType.DMA,
             pltpu.SemaphoreType.REGULAR,
+            pltpu.SMEM(dep_col.shape, jnp.int32),
+            pltpu.VMEM(lon_steps.shape, jnp.int32),
+            pltpu.VMEM(tilt_steps.shape, jnp.int32),
+            pltpu.SemaphoreType.DMA((3,)),
         ],
         compiler_params=pltpu.CompilerParams(
             collective_id=0, has_side_effects=True, vmem_limit_bytes=LIMIT
         ),
-    )(*[pltpu.with_memory_space_constraint(a, pltpu.HBM) for a in (pair_low, legendre, spectral)])
+    )(*[pltpu.with_memory_space_constraint(a, pltpu.HBM) for a in operands])
 
 
 def spread_low(low_ref):
@@ -312,14 +336,42 @@
                 order_ref[e, pl.ds(n0, 16), pl.ds(128 * v, 128)] = block.astype(bf16)
 
 
+def plan_into(index_ref, mix_ref, col_ref, lon_ref, tilt_ref):
+    lane = lax.broadcasted_iota(jnp.int32, (8, 128), 1)
+    hemi = lax.broadcasted_iota(jnp.int32, (8, 128), 0) % 2 == 1
+    for l in range(2):
+        for x in range(10):
+            north, south = 10 * l + x, 20 + 10 * l + x
+
+            def pick(ref):
+                return jnp.where(
+                    hemi,
+                    jnp.broadcast_to(ref[south : south + 1, :], (8, 128)),
+                    jnp.broadcast_to(ref[north : north + 1, :], (8, 128)),
+                )
+
+            lon, tilt = pick(lon_ref), pick(tilt_ref)
+
+            def shift_of(block):
+                return lax.rem(col_ref[block] - 128 * x + 1280 + 640, 1280) - 643
+
+            n = 10 * l + x
+            index_ref[n] = lane + jnp.where(hemi, shift_of(south), shift_of(north)) + (lon >> 2)
+            f = (lon & 3).astype(f32) * 0.25
+            g = (tilt & 3).astype(f32) * 0.25
+            mix_ref[n, 0] = (1.0 - g) * (1.0 - f)
+            mix_ref[n, 1] = (1.0 - g) * f
+            mix_ref[n, 2] = g * (1.0 - f)
+            mix_ref[n, 3] = g * f
+            mix_ref[n, 4] = (tilt >> 2).astype(f32) * 0.25
+
+
 def grid_kernel(
-    lat_ref, col_ref, recv_ref, order_ref, lon_ref, tilt_ref, table_hi_ref, table_lo_ref, twiddle_ref,
-    grid_ref, departed_ref, x_ref, field_ref, edge_ref, lat_smem, col_smem, lat_sem, col_sem, levs,
+    lat_ref, recv_ref, order_ref, index_ref, mix_ref, table_hi_ref, table_lo_ref, twiddle_ref,
+    grid_ref, departed_ref, x_ref, field_ref, edge_ref, lat_smem, lat_sem, levs,
 ):
     lat_copy = pltpu.make_async_copy(lat_ref, lat_smem, lat_sem)
     lat_copy.start()
-    col_copy = pltpu.make_async_copy(col_ref, col_smem, col_sem)
-    col_copy.start()
     wave = lax.axis_index("wave")
     last = lax.axis_index("lev") == levs - 1
 
@@ -415,49 +467,33 @@
                 grid_ref[lev, pl.ds(2 * h + l, 1), pl.ds(128 * x, 128)] = field_ref[x, pl.ds(8 * (2 + l) + row, 1), :]
 
     lat_copy.wait()
-    col_copy.wait()
     hemi = lax.broadcasted_iota(jnp.int32, (8, 128), 0) % 2 == 1
     keep_own = jnp.logical_and(last, lax.broadcasted_iota(jnp.int32, (8, 128), 0) >= 2)
     for l in range(2):
         for x in range(10):
             north, south = 10 * l + x, 20 + 10 * l + x
 
-            def pick(ref):
-                return jnp.where(
-                    hemi,
-                    jnp.broadcast_to(ref[south : south + 1, :], (8, 128)),
-                    jnp.broadcast_to(ref[north : north + 1, :], (8, 128)),
-                )
-
-            lon, tilt = pick(lon_ref), pick(tilt_ref)
-
-            def shift_of(block):
-                return lax.rem(col_smem[block] - 128 * x + 1280 + 640, 1280) - 640
-
-            base = jnp.where(hemi, shift_of(south), shift_of(north))
-            index = lane + base + (lon >> 2) - 3
+            n = 10 * l + x
+            index = index_ref[n]
             nxt = index + 1
-            frac = (lon & 3).astype(f32) * 0.25
-            g = (tilt & 3).astype(f32) * 0.25
-            v = (tilt >> 2).astype(f32) * 0.25
+            starts = [8 * (lat_smem[block] + (2 - 2 * wave)) for block in (north, south)]
             rows = []
             for off in range(2):
-                starts = [
-                    pl.multiple_of(8 * (lat_smem[block] - 2 * wave + 2 + off), 8) for block in (north, south)
-                ]
-                main = jnp.where(hemi, field_ref[x, pl.ds(starts[1], 8), :], field_ref[x, pl.ds(starts[0], 8), :])
-                edge = jnp.where(hemi, edge_ref[x, pl.ds(starts[1], 8), :], edge_ref[x, pl.ds(starts[0], 8), :])
-
-                def look(at):
-                    inside = (at >> 7) == 0
+                at = [pl.multiple_of(start + 8 * off, 8) for start in starts]
+                main = jnp.where(hemi, field_ref[x, pl.ds(at[1], 8), :], field_ref[x, pl.ds(at[0], 8), :])
+                edge = jnp.where(hemi, edge_ref[x, pl.ds(at[1], 8), :], edge_ref[x, pl.ds(at[0], 8), :])
+
+                def look(column):
+                    wrapped = column & 127
                     return jnp.where(
-                        inside,
-                        jnp.take_along_axis(main, at & 127, axis=1),
-                        jnp.take_along_axis(edge, at & 127, axis=1),
+                        wrapped == column,
+                        jnp.take_along_axis(main, wrapped, axis=1),
+                        jnp.take_along_axis(edge, wrapped, axis=1),
                     )
 
-                rows.append((1.0 - frac) * look(index) + frac * look(nxt))
-            horizontal = (1.0 - g) * rows[0] + g * rows[1]
+                rows.append(mix_ref[n, 2 * off] * look(index) + mix_ref[n, 2 * off + 1] * look(nxt))
+            horizontal = rows[0] + rows[1]
+            v = mix_ref[n, 4]
             upper = jnp.where(keep_own, horizontal, pltpu.roll(horizontal, 6, 0))
             departed = (1.0 - v) * horizontal + v * upper
             for row in range(4):
@@ -481,7 +517,7 @@
     return hi, lo, twiddle
 
 
-def to_grid(dep_lat, dep_col, received, order, lon_steps, tilt_steps, levs):
+def to_grid(dep_lat, received, order, index, mix, levs):
     hi, lo, twiddle = dft_tables()
     vmem = pl.BlockSpec(memory_space=pltpu.VMEM)
     outside = pl.BlockSpec(memory_space=pl.ANY)
@@ -492,27 +528,27 @@
     return pl.pallas_call(
         kernel,
         out_shape=[jax.ShapeDtypeStruct((2, 4, 1280), f32)] * 2,
-        in_specs=[outside, outside] + [vmem] * 7,
+        in_specs=[outside] + [vmem] * 7,
         out_specs=[vmem, vmem],
         scratch_shapes=[
             pltpu.VMEM((2, 192, 512), bf16),
             pltpu.VMEM((10, 48, 128), f32),
             pltpu.VMEM((10, 48, 128), f32),
             pltpu.SMEM(dep_lat.shape, jnp.int32),
-            pltpu.SMEM(dep_col.shape, jnp.int32),
-            pltpu.SemaphoreType.DMA,
             pltpu.SemaphoreType.DMA,
         ],
         compiler_params=pltpu.CompilerParams(vmem_limit_bytes=LIMIT),
         name="grid",
-    )(dep_lat, dep_col, received, order, lon_steps, tilt_steps, jnp.asarray(hi), jnp.asarray(lo), jnp.asarray(twiddle))
+    )(dep_lat, received, order, index, mix, jnp.asarray(hi), jnp.asarray(lo), jnp.asarray(twiddle))
 
 
 def per_device(legendre, spectral, pair_low, dep_lat, dep_col, lon_steps, tilt_steps):
     waves, levs = lax.axis_size("wave"), lax.axis_size("lev")
-    received, order = exchange(pair_low, legendre, spectral, waves, levs)
+    received, order, index, mix = exchange(
+        pair_low, legendre, spectral, dep_col, lon_steps, tilt_steps, waves, levs
+    )
     received = received.reshape(waves, 3, 8, 128)
-    return tuple(to_grid(dep_lat, dep_col, received, order, lon_steps, tilt_steps, levs))
+    return tuple(to_grid(dep_lat, received, order, index, mix, levs))
 
 
 def solution(mesh):

time: 22.4 us -> 22.2 us (level)
    pallas_call x1, Pallas kernels: 2.29 us -> 2.05 us  [to_grid(): pl.pallas_call(kernel, out_shape=[jax.ShapeDtypeStruct((2, 4, 1280), f32)...]
where the time goes in v5:
time: 22.2 us; the launch traced here: 22 us
  Pallas kernels  21.3 us (96%)
  between operations  0.7 us (3%)
    pallas_call x1, Pallas kernels, exchange(): pl.pallas_call(functools.partial(exchange_kernel, waves, levs), out_shape...  19.2 us
    pallas_call x1, Pallas kernels, to_grid(): pl.pallas_call(kernel, out_shape=[jax.ShapeDtypeStruct((2, 4, 1280), f32)...  2.05 us

profile of v5, /device:TPU:27, one launch (start us, length us, event | category | flops | bytes accessed | tf_op | source)
XLA Modules:
  0.0 22.0 jit_solution(10217482224167421525)
XLA Ops:
  0.6 0.0 copy-start.2
  0.6 0.0 copy-start
  0.7 0.0 copy-start.1
  0.7 0.0 copy-start.3
  0.7 19.2 %shard_map.113 = (f32[32,3,4,2,128]{4,3,2,1,0:T(2,128)S(1)}, bf16[2,384,512]{2,1,0:T(8,128)(2,1)S(1)}, s32[20,8,128]{2,1,0:T(8,128)S(1)}, f32[20,5,8,128]{3,2,1,0:T(8,128)S(1)}) custom-call(s32[320]{0:T(512)} %low_hbm.1, f32[10,64,641]{2,1,0:T(8,128)} %leg_hbm.1, f32[10,2,2,641]{3,2,1,0:T(2,128)} %spec_hbm.1, s32[40]{0:T(128)} %col_hbm.1, ...), custom_call_target="tpu_custom_call" | custom-call | tf_op jit(solution)/shard_map/pallas_call | solution.py:254
  19.9 0.0 copy-done.2
  19.9 0.0 copy-done
  19.9 0.0 copy-done.1
  19.9 0.0 copy-done.3
  19.9 2.1 %grid.1 = (f32[2,4,1280]{2,1,0:T(4,128)}, f32[2,4,1280]{2,1,0:T(4,128)}) custom-call(s32[40]{0:T(128)S(1)} %copy-done.3, f32[32,3,8,128]{3,2,1,0:T(8,128)S(1)} %bitcast.1, bf16[2,384,512]{2,1,0:T(8,128)(2,1)S(1)} %get-tuple-element.7.refs_2_, s32[20,8,128]{2,1,0:T(8,128)S(1)} %get-tuple-element.8.refs_3_, f32[20,5,8,128]{3,2,1,0:T(8,128)S(1)} %get-tuple-element.9.refs_4_, ...), custom_call_target="tpu_custom_call" | custom-call | tf_op jit(solution)/shard_map/grid/pallas_call | solution.py:528
Async XLA Ops:
  0.6 19.3 %copy-start.2 = (f32[20,128]{1,0:T(8,128)S(1)}, f32[20,128]{1,0:T(8,128)}, u32[]{:S(2)}) copy-start(f32[20,128]{1,0:T(8,128)} %constant.8.clone.refs_7_) | copy-start | bytes 30724
  0.6 19.3 %copy-start = (bf16[224,256]{1,0:T(8,128)(2,1)S(1)}, bf16[224,256]{1,0:T(8,128)(2,1)}, u32[]{:S(2)}) copy-start(bf16[224,256]{1,0:T(8,128)(2,1)} %constant.7.clone.refs_6_) | copy-start | bytes 344068
  0.7 19.3 %copy-start.1 = (bf16[224,256]{1,0:T(8,128)(2,1)S(1)}, bf16[224,256]{1,0:T(8,128)(2,1)}, u32[]{:S(2)}) copy-start(bf16[224,256]{1,0:T(8,128)(2,1)} %constant.6.clone.refs_5_) | copy-start | bytes 344068
  0.7 19.3 %copy-start.3 = (s32[40]{0:T(128)S(1)}, s32[40]{0:T(128)}, u32[]{:S(2)}) copy-start(s32[40]{0:T(128)} %refs_0_.1) | copy-start | bytes 484

commit v6 on v5

--- a/solution.py
+++ b/solution.py
@@ -83,11 +83,8 @@
     low_copy.start()
     spec_copy = pltpu.make_async_copy(spec_hbm, spec_ref, spec_sem)
     spec_copy.start()
-    leg_copies = [
-        pltpu.make_async_copy(leg_hbm.at[s], leg_ref.at[s], leg_sem.at[s]) for s in range(pairs)
-    ]
-    for copy in leg_copies:
-        copy.start()
+    for s in range(0, pairs, 2):
+        pltpu.make_async_copy(leg_hbm.at[pl.ds(s, 2)], leg_ref.at[pl.ds(s, 2)], leg_sem).start()
     low_again = pltpu.make_async_copy(low_hbm, low_vmem, low_sem.at[1])
     low_again.start()
     plan_copies = [
@@ -130,8 +127,7 @@
     def wait_pair(s):
         if s == 0:
             spec_copy.wait()
-            for copy in leg_copies:
-                copy.wait()
+            pltpu.make_async_copy(leg_hbm, leg_ref, leg_sem).wait()
 
     legendre_into(
         send_ref, lambda s: low_smem[me * pairs + s], leg_ref, spec_ref, wait_pair, y_ref, z_ref,
@@ -162,14 +158,24 @@
             device_id_type=MESH,
         ).start()
 
+    def turn(quarter):
+        return jnp.where(quarter == 0, 0, jnp.where(quarter == 1, 3, quarter - 1))
+
     def spread(d):
-        peer = lax.rem(me + waves // 2 + d, waves)
-
-        @pl.when(jnp.logical_and(peer != 0, peer != me))
+        peer = lax.rem(me + 8 * turn(d // 8) + d % 8, waves)
+
+        @pl.when(peer != 0)
         def _():
             across(peer, recv_ref, peer, recv_sem)
 
-    each(0, spread)
+    @pl.when(late)
+    def _():
+        for peer in [*range(1, 8), *range(24, 32), *range(8, 24)]:
+            across(peer, recv_ref, peer, recv_sem)
+
+    @pl.when(jnp.logical_not(late))
+    def _():
+        each(1, spread)
 
     @pl.when(me > 1)
     def _():
@@ -270,7 +276,7 @@
             pltpu.VMEM((lats, 128), f32),
             pltpu.VMEM((lats // 2 + 2, 2, 2, 128), f32),
             pltpu.SemaphoreType.DMA((2,)),
-            pltpu.SemaphoreType.DMA((pairs,)),
+            pltpu.SemaphoreType.DMA,
             pltpu.SemaphoreType.DMA,
             pltpu.SemaphoreType.DMA,
             pltpu.SemaphoreType.DMA,

time: 22.2 us -> 22.1 us (level)
  the two profiles are of different devices: /device:TPU:27 before, /device:TPU:29 now
where the time goes in v6:
time: 22.1 us; the launch traced here: 21.9 us
  Pallas kernels  21.2 us (96%)
  between operations  0.7 us (3%)
    pallas_call x1, Pallas kernels, exchange(): pl.pallas_call(functools.partial(exchange_kernel, waves, levs), out_shape...  19.1 us
    pallas_call x1, Pallas kernels, to_grid(): pl.pallas_call(kernel, out_shape=[jax.ShapeDtypeStruct((2, 4, 1280), f32)...  2.04 us

profile of v6, /device:TPU:29, one launch (start us, length us, event | category | flops | bytes accessed | tf_op | source)
XLA Modules:
  0.0 21.9 jit_solution(12043910292008308611)
XLA Ops:
  0.6 0.0 copy-start.2
  0.6 0.0 copy-start
  0.7 0.0 copy-start.1
  0.7 0.0 copy-start.3
  0.7 19.1 %shard_map.113 = (f32[32,3,4,2,128]{4,3,2,1,0:T(2,128)S(1)}, bf16[2,384,512]{2,1,0:T(8,128)(2,1)S(1)}, s32[20,8,128]{2,1,0:T(8,128)S(1)}, f32[20,5,8,128]{3,2,1,0:T(8,128)S(1)}) custom-call(s32[320]{0:T(512)} %low_hbm.1, f32[10,64,641]{2,1,0:T(8,128)} %leg_hbm.1, f32[10,2,2,641]{3,2,1,0:T(2,128)} %spec_hbm.1, s32[40]{0:T(128)} %col_hbm.1, ...), custom_call_target="tpu_custom_call" | custom-call | tf_op jit(solution)/shard_map/pallas_call | solution.py:260
  19.8 0.0 copy-done.2
  19.8 0.0 copy-done
  19.8 0.0 copy-done.1
  19.8 0.0 copy-done.3
  19.9 2.0 %grid.1 = (f32[2,4,1280]{2,1,0:T(4,128)}, f32[2,4,1280]{2,1,0:T(4,128)}) custom-call(s32[40]{0:T(128)S(1)} %copy-done.3, f32[32,3,8,128]{3,2,1,0:T(8,128)S(1)} %bitcast.1, bf16[2,384,512]{2,1,0:T(8,128)(2,1)S(1)} %get-tuple-element.7.refs_2_, s32[20,8,128]{2,1,0:T(8,128)S(1)} %get-tuple-element.8.refs_3_, f32[20,5,8,128]{3,2,1,0:T(8,128)S(1)} %get-tuple-element.9.refs_4_, ...), custom_call_target="tpu_custom_call" | custom-call | tf_op jit(solution)/shard_map/grid/pallas_call | solution.py:534
Async XLA Ops:
  0.6 19.2 %copy-start.2 = (f32[20,128]{1,0:T(8,128)S(1)}, f32[20,128]{1,0:T(8,128)}, u32[]{:S(2)}) copy-start(f32[20,128]{1,0:T(8,128)} %constant.8.clone.refs_7_) | copy-start | bytes 30724
  0.6 19.2 %copy-start = (bf16[224,256]{1,0:T(8,128)(2,1)S(1)}, bf16[224,256]{1,0:T(8,128)(2,1)}, u32[]{:S(2)}) copy-start(bf16[224,256]{1,0:T(8,128)(2,1)} %constant.7.clone.refs_6_) | copy-start | bytes 344068
  0.7 19.2 %copy-start.1 = (bf16[224,256]{1,0:T(8,128)(2,1)S(1)}, bf16[224,256]{1,0:T(8,128)(2,1)}, u32[]{:S(2)}) copy-start(bf16[224,256]{1,0:T(8,128)(2,1)} %constant.6.clone.refs_5_) | copy-start | bytes 344068
  0.7 19.2 %copy-start.3 = (s32[40]{0:T(128)S(1)}, s32[40]{0:T(128)}, u32[]{:S(2)}) copy-start(s32[40]{0:T(128)} %refs_0_.1) | copy-start | bytes 484

commit v7 on v6

--- a/solution.py
+++ b/solution.py
@@ -11,6 +11,7 @@
 
 MESH = pl.DeviceIdType.MESH
 LIMIT = 16 * 1024 * 1024
+ORDER = (2, 3, 28, 29, 12, 13, 20, 21, 30, 31, 10, 11, 14, 15, 26, 27, 6, 7, 24, 25, 8, 9, 22, 23, 18, 19, 1, 4, 5, 16, 17)
 NT = (((1,), (1,)), ((), ()))
 f32 = jnp.float32
 bf16 = jnp.bfloat16
@@ -43,15 +44,19 @@
         first = top - low_of(s)
         keep = signed_k >= jnp.where(second, first, 1 - first)
         mask = jnp.where(keep, jnp.where((first & 1) == 0, sign_even, sign_odd), 0.0)
-        rows = []
-        for lev in range(2):
-            re = jnp.broadcast_to(spec_ref[s, lev, 0:1, :], (8, slots))
-            im = jnp.broadcast_to(spec_ref[s, lev, 1:2, :], (8, slots))
-            rows.append(jnp.where(real, re, im) * mask)
-        hi, lo = split(jnp.concatenate(rows, axis=0))
-        leg_hi, leg_lo = split(leg_ref[s])
-        both = lax.dot_general(jnp.concatenate([hi, lo], axis=0), leg_hi, NT, preferred_element_type=f32)
-        small = lax.dot_general(hi, leg_lo, NT, preferred_element_type=f32)
+        both, small = None, None
+        for a, b in ((0, 256), (256, 512), (512, slots)):
+            rows = []
+            for lev in range(2):
+                re = jnp.broadcast_to(spec_ref[s, lev, 0:1, a:b], (8, b - a))
+                im = jnp.broadcast_to(spec_ref[s, lev, 1:2, a:b], (8, b - a))
+                rows.append(jnp.where(real[:, a:b], re, im) * mask[:, a:b])
+            hi, lo = split(jnp.concatenate(rows, axis=0))
+            leg_hi, leg_lo = split(leg_ref[s, :, a:b])
+            d1 = lax.dot_general(jnp.concatenate([hi, lo], axis=0), leg_hi, NT, preferred_element_type=f32)
+            d2 = lax.dot_general(hi, leg_lo, NT, preferred_element_type=f32)
+            both = d1 if both is None else both + d1
+            small = d2 if small is None else small + d2
         y_ref[pl.ds(s, 16, stride=16), :] = both[:16] + (both[16:] + small)
     lane = lax.broadcasted_iota(jnp.int32, (lats // 2, 128), 1)
     for lev in range(2):
@@ -170,7 +175,7 @@
 
     @pl.when(late)
     def _():
-        for peer in [*range(1, 8), *range(24, 32), *range(8, 24)]:
+        for peer in ORDER:
             across(peer, recv_ref, peer, recv_sem)
 
     @pl.when(jnp.logical_not(late))

time: 22.1 us -> 22.3 us (level)
  the two profiles are of different devices: /device:TPU:29 before, /device:TPU:5 now
where the time goes in v7:
time: 22.3 us; the launch traced here: 22.2 us
  Pallas kernels  21.4 us (96%)
  between operations  0.7 us (3%)
    pallas_call x1, Pallas kernels, exchange(): pl.pallas_call(functools.partial(exchange_kernel, waves, levs), out_shape...  19.4 us
    pallas_call x1, Pallas kernels, to_grid(): pl.pallas_call(kernel, out_shape=[jax.ShapeDtypeStruct((2, 4, 1280), f32)...  2.05 us

profile of v7, /device:TPU:5, one launch (start us, length us, event | category | flops | bytes accessed | tf_op | source)
XLA Modules:
  0.0 22.2 jit_solution(7363061939463743092)
XLA Ops:
  0.6 0.0 copy-start.2
  0.6 0.0 copy-start
  0.7 0.0 copy-start.1
  0.7 0.0 copy-start.3
  0.7 19.4 %shard_map.113 = (f32[32,3,4,2,128]{4,3,2,1,0:T(2,128)S(1)}, bf16[2,384,512]{2,1,0:T(8,128)(2,1)S(1)}, s32[20,8,128]{2,1,0:T(8,128)S(1)}, f32[20,5,8,128]{3,2,1,0:T(8,128)S(1)}) custom-call(s32[320]{0:T(512)} %low_hbm.1, f32[10,64,641]{2,1,0:T(8,128)} %leg_hbm.1, f32[10,2,2,641]{3,2,1,0:T(2,128)} %spec_hbm.1, s32[40]{0:T(128)} %col_hbm.1, ...), custom_call_target="tpu_custom_call" | custom-call | tf_op jit(solution)/shard_map/pallas_call | solution.py:265
  20.1 0.0 copy-done.2
  20.1 0.0 copy-done
  20.1 0.0 copy-done.1
  20.1 0.0 copy-done.3
  20.1 2.0 %grid.1 = (f32[2,4,1280]{2,1,0:T(4,128)}, f32[2,4,1280]{2,1,0:T(4,128)}) custom-call(s32[40]{0:T(128)S(1)} %copy-done.3, f32[32,3,8,128]{3,2,1,0:T(8,128)S(1)} %bitcast.1, bf16[2,384,512]{2,1,0:T(8,128)(2,1)S(1)} %get-tuple-element.7.refs_2_, s32[20,8,128]{2,1,0:T(8,128)S(1)} %get-tuple-element.8.refs_3_, f32[20,5,8,128]{3,2,1,0:T(8,128)S(1)} %get-tuple-element.9.refs_4_, ...), custom_call_target="tpu_custom_call" | custom-call | tf_op jit(solution)/shard_map/grid/pallas_call | solution.py:539
Async XLA Ops:
  0.6 19.4 %copy-start.2 = (f32[20,128]{1,0:T(8,128)S(1)}, f32[20,128]{1,0:T(8,128)}, u32[]{:S(2)}) copy-start(f32[20,128]{1,0:T(8,128)} %constant.8.clone.refs_7_) | copy-start | bytes 30724
  0.6 19.4 %copy-start = (bf16[224,256]{1,0:T(8,128)(2,1)S(1)}, bf16[224,256]{1,0:T(8,128)(2,1)}, u32[]{:S(2)}) copy-start(bf16[224,256]{1,0:T(8,128)(2,1)} %constant.7.clone.refs_6_) | copy-start | bytes 344068
  0.7 19.4 %copy-start.1 = (bf16[224,256]{1,0:T(8,128)(2,1)S(1)}, bf16[224,256]{1,0:T(8,128)(2,1)}, u32[]{:S(2)}) copy-start(bf16[224,256]{1,0:T(8,128)(2,1)} %constant.6.clone.refs_5_) | copy-start | bytes 344068
  0.7 19.4 %copy-start.3 = (s32[40]{0:T(128)S(1)}, s32[40]{0:T(128)}, u32[]{:S(2)}) copy-start(s32[40]{0:T(128)} %refs_0_.1) | copy-start | bytes 484

commit v8 on v7

--- a/solution.py
+++ b/solution.py
@@ -11,7 +11,7 @@
 
 MESH = pl.DeviceIdType.MESH
 LIMIT = 16 * 1024 * 1024
-ORDER = (2, 3, 28, 29, 12, 13, 20, 21, 30, 31, 10, 11, 14, 15, 26, 27, 6, 7, 24, 25, 8, 9, 22, 23, 18, 19, 1, 4, 5, 16, 17)
+ORDER = (28, 29, 4, 5, 12, 13, 20, 21, 2, 3, 30, 31, 10, 11, 14, 15, 6, 7, 26, 27, 24, 25, 8, 9, 22, 23, 18, 19, 1, 16, 17)
 NT = (((1,), (1,)), ((), ()))
 f32 = jnp.float32
 bf16 = jnp.bfloat16

time: 22.3 us -> 22.3 us (level)
  no operation moved by 1% of the time
where the time goes in v8:
time: 22.3 us; the launch traced here: 22.2 us
  Pallas kernels  21.4 us (96%)
  between operations  0.7 us (3%)
    pallas_call x1, Pallas kernels, exchange(): pl.pallas_call(functools.partial(exchange_kernel, waves, levs), out_shape...  19.4 us
    pallas_call x1, Pallas kernels, to_grid(): pl.pallas_call(kernel, out_shape=[jax.ShapeDtypeStruct((2, 4, 1280), f32)...  2.05 us

profile of v8, /device:TPU:5, one launch (start us, length us, event | category | flops | bytes accessed | tf_op | source)
XLA Modules:
  0.0 22.2 jit_solution(2384466619989346710)
XLA Ops:
  0.6 0.0 copy-start.2
  0.6 0.0 copy-start
  0.7 0.0 copy-start.1
  0.7 0.0 copy-start.3
  0.7 19.4 %shard_map.113 = (f32[32,3,4,2,128]{4,3,2,1,0:T(2,128)S(1)}, bf16[2,384,512]{2,1,0:T(8,128)(2,1)S(1)}, s32[20,8,128]{2,1,0:T(8,128)S(1)}, f32[20,5,8,128]{3,2,1,0:T(8,128)S(1)}) custom-call(s32[320]{0:T(512)} %low_hbm.1, f32[10,64,641]{2,1,0:T(8,128)} %leg_hbm.1, f32[10,2,2,641]{3,2,1,0:T(2,128)} %spec_hbm.1, s32[40]{0:T(128)} %col_hbm.1, ...), custom_call_target="tpu_custom_call" | custom-call | tf_op jit(solution)/shard_map/pallas_call | solution.py:265
  20.1 0.0 copy-done.2
  20.1 0.0 copy-done
  20.1 0.0 copy-done.1
  20.1 0.0 copy-done.3
  20.1 2.0 %grid.1 = (f32[2,4,1280]{2,1,0:T(4,128)}, f32[2,4,1280]{2,1,0:T(4,128)}) custom-call(s32[40]{0:T(128)S(1)} %copy-done.3, f32[32,3,8,128]{3,2,1,0:T(8,128)S(1)} %bitcast.1, bf16[2,384,512]{2,1,0:T(8,128)(2,1)S(1)} %get-tuple-element.7.refs_2_, s32[20,8,128]{2,1,0:T(8,128)S(1)} %get-tuple-element.8.refs_3_, f32[20,5,8,128]{3,2,1,0:T(8,128)S(1)} %get-tuple-element.9.refs_4_, ...), custom_call_target="tpu_custom_call" | custom-call | tf_op jit(solution)/shard_map/grid/pallas_call | solution.py:539
Async XLA Ops:
  0.6 19.4 %copy-start.2 = (f32[20,128]{1,0:T(8,128)S(1)}, f32[20,128]{1,0:T(8,128)}, u32[]{:S(2)}) copy-start(f32[20,128]{1,0:T(8,128)} %constant.8.clone.refs_7_) | copy-start | bytes 30724
  0.6 19.4 %copy-start = (bf16[224,256]{1,0:T(8,128)(2,1)S(1)}, bf16[224,256]{1,0:T(8,128)(2,1)}, u32[]{:S(2)}) copy-start(bf16[224,256]{1,0:T(8,128)(2,1)} %constant.7.clone.refs_6_) | copy-start | bytes 344068
  0.7 19.4 %copy-start.1 = (bf16[224,256]{1,0:T(8,128)(2,1)S(1)}, bf16[224,256]{1,0:T(8,128)(2,1)}, u32[]{:S(2)}) copy-start(bf16[224,256]{1,0:T(8,128)(2,1)} %constant.6.clone.refs_5_) | copy-start | bytes 344068
  0.7 19.4 %copy-start.3 = (s32[40]{0:T(128)S(1)}, s32[40]{0:T(128)}, u32[]{:S(2)}) copy-start(s32[40]{0:T(128)} %refs_0_.1) | copy-start | bytes 484

commit v9 on v8

--- a/solution.py
+++ b/solution.py
@@ -233,12 +233,6 @@
         def _():
             relay(downs, relay_down_sem, down_recv_sem).start()
 
-    wait_for(recv_ref.at[:, :, pl.ds(0, 2)], recv_sem)
-
-    @pl.when(upper)
-    def _():
-        wait_for(downs(recv_ref), down_recv_sem)
-
     @pl.when(me == 1)
     def _():
         wait_for(others(proxy_ref), relay_sem)
@@ -255,6 +249,12 @@
     @pl.when(lower)
     def _():
         wait_for(downs(recv_ref), down_send_sem)
+
+    @pl.when(upper)
+    def _():
+        wait_for(downs(recv_ref), down_recv_sem)
+
+    wait_for(recv_ref.at[:, :, pl.ds(0, 2)], recv_sem)
 
 
 def exchange(pair_low, legendre, spectral, dep_col, lon_steps, tilt_steps, waves, levs):

time: 22.3 us -> 22.3 us (level)
  no operation moved by 1% of the time
where the time goes in v9:
time: 22.3 us; the launch traced here: 22.1 us
  Pallas kernels  21.4 us (96%)
  between operations  0.7 us (3%)
    pallas_call x1, Pallas kernels, exchange(): pl.pallas_call(functools.partial(exchange_kernel, waves, levs), out_shape...  19.4 us
    pallas_call x1, Pallas kernels, to_grid(): pl.pallas_call(kernel, out_shape=[jax.ShapeDtypeStruct((2, 4, 1280), f32)...  2.05 us

profile of v9, /device:TPU:5, one launch (start us, length us, event | category | flops | bytes accessed | tf_op | source)
XLA Modules:
  0.0 22.1 jit_solution(2433624367541274133)
XLA Ops:
  0.6 0.0 copy-start.2
  0.6 0.0 copy-start
  0.7 0.0 copy-start.1
  0.7 0.0 copy-start.3
  0.7 19.4 %shard_map.113 = (f32[32,3,4,2,128]{4,3,2,1,0:T(2,128)S(1)}, bf16[2,384,512]{2,1,0:T(8,128)(2,1)S(1)}, s32[20,8,128]{2,1,0:T(8,128)S(1)}, f32[20,5,8,128]{3,2,1,0:T(8,128)S(1)}) custom-call(s32[320]{0:T(512)} %low_hbm.1, f32[10,64,641]{2,1,0:T(8,128)} %leg_hbm.1, f32[10,2,2,641]{3,2,1,0:T(2,128)} %spec_hbm.1, s32[40]{0:T(128)} %col_hbm.1, ...), custom_call_target="tpu_custom_call" | custom-call | tf_op jit(solution)/shard_map/pallas_call | solution.py:265
  20.1 0.0 copy-done.2
  20.1 0.0 copy-done
  20.1 0.0 copy-done.1
  20.1 0.0 copy-done.3
  20.1 2.1 %grid.1 = (f32[2,4,1280]{2,1,0:T(4,128)}, f32[2,4,1280]{2,1,0:T(4,128)}) custom-call(s32[40]{0:T(128)S(1)} %copy-done.3, f32[32,3,8,128]{3,2,1,0:T(8,128)S(1)} %bitcast.1, bf16[2,384,512]{2,1,0:T(8,128)(2,1)S(1)} %get-tuple-element.7.refs_2_, s32[20,8,128]{2,1,0:T(8,128)S(1)} %get-tuple-element.8.refs_3_, f32[20,5,8,128]{3,2,1,0:T(8,128)S(1)} %get-tuple-element.9.refs_4_, ...), custom_call_target="tpu_custom_call" | custom-call | tf_op jit(solution)/shard_map/grid/pallas_call | solution.py:539
Async XLA Ops:
  0.6 19.4 %copy-start.2 = (f32[20,128]{1,0:T(8,128)S(1)}, f32[20,128]{1,0:T(8,128)}, u32[]{:S(2)}) copy-start(f32[20,128]{1,0:T(8,128)} %constant.8.clone.refs_7_) | copy-start | bytes 30724
  0.6 19.4 %copy-start = (bf16[224,256]{1,0:T(8,128)(2,1)S(1)}, bf16[224,256]{1,0:T(8,128)(2,1)}, u32[]{:S(2)}) copy-start(bf16[224,256]{1,0:T(8,128)(2,1)} %constant.7.clone.refs_6_) | copy-start | bytes 344068
  0.7 19.4 %copy-start.1 = (bf16[224,256]{1,0:T(8,128)(2,1)S(1)}, bf16[224,256]{1,0:T(8,128)(2,1)}, u32[]{:S(2)}) copy-start(bf16[224,256]{1,0:T(8,128)(2,1)} %constant.6.clone.refs_5_) | copy-start | bytes 344068
  0.7 19.4 %copy-start.3 = (s32[40]{0:T(128)S(1)}, s32[40]{0:T(128)}, u32[]{:S(2)}) copy-start(s32[40]{0:T(128)} %refs_0_.1) | copy-start | bytes 484
